TPU v7x, 512 devices: a whole 4x4x16 slice. The times are simulated.
512 devices in a mesh: fsdp: 32 (over y, z_hi, x), tensor: 16 (over z_lo, core).
Axes of the slice: x: 4, y: 4, z: 16 (z_hi: 2, z_lo: 8; z = z_hi * 8 + z_lo), core: 2. Of those that a mesh axis runs over, the one named last changes fastest.
Arguments:
- tokens: bfloat16 [512, 9216], P(None, 'tensor'), may hold values from -800 to 800
- ln_gain: bfloat16 [9216], P('tensor'), may hold values from 0.099609375 to 1.8984375
- ln_bias: bfloat16 [9216], P('tensor'), may hold values from -3 to 3
- fc1_weight: bfloat16 [9216, 36864], P('tensor', 'fsdp'), may hold values from -0.0625 to 0.0625
- fc1_bias: bfloat16 [36864], P('fsdp'), may hold values from -3 to 3
- fc2_weight: bfloat16 [36864, 9216], P('fsdp', 'tensor'), may hold values from -0.03125 to 0.03125
- fc2_bias: bfloat16 [9216], P('tensor'), may hold values from -3 to 3
- update_step: float32 [1], replicated, may hold values from -0.004 to 0.004
- perturb_scale: float32 [1], replicated, may hold values from 0.002 to 0.008
- step_seeds: int32 [2], replicated, may hold values from 0 to 16777215
- hash_mults: int32 [3], replicated, may hold values from 65537 to 16777215
Outputs:
- branch_plus: bfloat16 [512, 9216], P('fsdp', 'tensor')
- branch_minus: bfloat16 [512, 9216], P('fsdp', 'tensor')
Inputs may be any that keep to these rules, and one draw needn't show every extreme that they name: `step_seeds`: the previous step's seed, then this step's. `hash_mults`: three multipliers; the lowest bit is set before use.
All inputs are finite; a program needn't handle non-finite values.
Results may differ from a plain program's by a relative error of at most 0.03.
Values may be sent and summed in bfloat16 or wider, within the bound.
No kernel may reach another device: no remote copies, remote signals or barrier semaphores. Data moves between devices by JAX's collectives and lax.ppermute only.
A program may use at most 64 MiB of HBM per device.

v0:
```python
import jax
import jax.numpy as jnp
from jax import lax
from jax.sharding import PartitionSpec as P

D = 9216
FF = 36864


def shift_xor(hashed, amount):
    return hashed ^ lax.shift_right_logical(hashed, jnp.int32(amount))


def hashed_noise(param_index, seed_value, hash_mults):
    mult_a = hash_mults[0] | 1
    mult_b = hash_mults[1] | 1
    mult_c = hash_mults[2] | 1
    hashed = param_index * mult_a + seed_value * mult_b
    hashed = shift_xor(hashed, 16)
    hashed = hashed * mult_c
    hashed = shift_xor(hashed, 13)
    hashed = hashed * mult_a
    hashed = shift_xor(hashed, 16)
    fraction = (hashed & 16777215).astype(jnp.float32) * (1.0 / 16777216.0)
    return (fraction - 0.5) * 3.4641016151377544


def new_weights(weight, param_index, update_step, perturb_scale, step_seeds, hash_mults):
    updated = (
        weight.astype(jnp.float32)
        - update_step[0] * hashed_noise(param_index, step_seeds[0], hash_mults)
    ).astype(jnp.bfloat16)
    updated = lax.optimization_barrier(updated)
    updated_f = updated.astype(jnp.float32)
    shift_term = perturb_scale[0] * hashed_noise(param_index, step_seeds[1], hash_mults)
    return (
        (updated_f + shift_term).astype(jnp.bfloat16),
        (updated_f - shift_term).astype(jnp.bfloat16),
    )


def body(
    tokens,
    ln_gain,
    ln_bias,
    fc1_weight,
    fc1_bias,
    fc2_weight,
    fc2_bias,
    update_step,
    perturb_scale,
    step_seeds,
    hash_mults,
):
    feat_local = tokens.shape[1]
    unit_local = fc1_weight.shape[1]
    values = tokens.astype(jnp.float32)
    totals = lax.psum(jnp.sum(values, axis=1), "tensor")
    row_mean = (totals / D)[:, None]
    centered = values - row_mean
    squares = lax.psum(jnp.sum(centered * centered, axis=1), "tensor")
    row_var = (squares / D)[:, None]
    normed = (
        centered * lax.rsqrt(row_var + 1e-05) * ln_gain.astype(jnp.float32)
        + ln_bias.astype(jnp.float32)
    ).astype(jnp.bfloat16)
    feat_ids = lax.axis_index("tensor") * feat_local + jnp.arange(feat_local, dtype=jnp.int32)
    unit_ids = lax.axis_index("fsdp") * unit_local + jnp.arange(unit_local, dtype=jnp.int32)
    first_index = feat_ids[:, None] * FF + unit_ids[None, :]
    plus_one, minus_one = new_weights(
        fc1_weight, first_index, update_step, perturb_scale, step_seeds, hash_mults
    )
    partial_plus = jnp.dot(normed, plus_one, preferred_element_type=jnp.float32)
    partial_minus = jnp.dot(normed, minus_one, preferred_element_type=jnp.float32)
    bias_one = fc1_bias.astype(jnp.float32)
    sum_plus, sum_minus = (
        lax.psum(partial_plus.astype(jnp.bfloat16), "tensor").astype(jnp.float32),
        lax.psum(partial_minus.astype(jnp.bfloat16), "tensor").astype(jnp.float32),
    )
    hidden_plus = jax.nn.relu(sum_plus + bias_one).astype(jnp.bfloat16)
    hidden_minus = jax.nn.relu(sum_minus + bias_one).astype(jnp.bfloat16)
    second_index = D * FF + unit_ids[:, None] * D + feat_ids[None, :]
    plus_two, minus_two = new_weights(
        fc2_weight, second_index, update_step, perturb_scale, step_seeds, hash_mults
    )
    summed = lax.psum_scatter(
        jnp.concatenate(
            [
                jnp.dot(hidden_plus, plus_two, preferred_element_type=jnp.float32),
                jnp.dot(hidden_minus, minus_two, preferred_element_type=jnp.float32),
            ],
            axis=1,
        ).astype(jnp.bfloat16),
        "fsdp",
        scatter_dimension=0,
        tiled=True,
    ).astype(jnp.float32)
    bias_two = fc2_bias.astype(jnp.float32)
    branch_plus = (summed[:, :feat_local] + bias_two).astype(jnp.bfloat16)
    branch_minus = (summed[:, feat_local:] + bias_two).astype(jnp.bfloat16)
    return (branch_plus, branch_minus)


def solution(mesh):
    in_specs = (
        P(None, "tensor"),
        P("tensor"),
        P("tensor"),
        P("tensor", "fsdp"),
        P("fsdp"),
        P("fsdp", "tensor"),
        P("tensor"),
        P(),
        P(),
        P(),
        P(),
    )
    out_specs = (P("fsdp", "tensor"), P("fsdp", "tensor"))
    return jax.shard_map(body, mesh=mesh, in_specs=in_specs, out_specs=out_specs, check_vma=False)
```

profile of v0, /device:TPU:1, one launch (start us, length us, event | category | flops | bytes accessed | tf_op | source)
XLA Modules:
  0.0 657.9 jit_solution(10783687590641612165)
XLA Ops:
  7.2 0.0 all-reduce.3.cloned.1.call-start
  7.2 1.3 fusion.107
  10.4 1.3 fusion.106
  13.0 0.0 copy-start
  13.1 0.0 copy-start.3
  13.1 0.0 copy-start.4
  13.1 3.2 fusion.35
  16.8 0.0 copy-done
  16.8 0.1 convert_reduce_fusion
  17.0 51.4 %psum.28 = f32[512]{0:T(512)S(1)} all-reduce(f32[512]{0:T(512)S(1)} %convert_reduce_fusion), channel_id=1, replica_groups=mesh['fsdp'=32,'tensor'=16] {'tensor'}, use_global_device_ids=true, to_apply=%region_1.0 | all-reduce | flops 512 | bytes 4096 | tf_op jit(solution)/shard_map/psum | solution.py:58
  68.3 0.2 fusion.72
  68.5 50.4 %psum.29 = f32[512]{0:T(512)S(1)} all-reduce(f32[512]{0:T(512)S(1)} %fusion.72), channel_id=1, replica_groups=mesh['fsdp'=32,'tensor'=16] {'tensor'}, use_global_device_ids=true, to_apply=%region_3.0 | all-reduce | flops 512 | bytes 4096 | tf_op jit(solution)/shard_map/psum | solution.py:61
  119.6 0.0 copy-done.3
  119.6 0.0 copy-done.4
  119.6 3.4 convolution_convert_fusion
  123.0 3.3 convolution_convert_fusion.1
  126.3 0.0 all-reduce.3.cloned.1.call-update
  126.4 0.2 reduce-scatter.4.cloned.1.call-start
  126.6 1.0 copy-done.1
  127.7 1.8 fusion.34
  129.5 199.1 %all-reduce.3.cloned.1.call-done = (bf16[512,1152]{1,0:T(8,128)(2,1)}, bf16[512,1152]{1,0:T(8,128)(2,1)}) async-done(((bf16[512,1152]{1,0:T(8,128)(2,1)}, bf16[512,1152]{1,0:T(8,128)(2,1)}), (bf16[512,1152]{1,0:T(8,128)(2,1)}, bf16[512,1152]{1,0:T(8,128)(2,1)})) %all-reduce.3.cloned.1.call-update) | async-done | bytes 2359312 | tf_op jit(solution)/shard_map/psum | solution.py:78
  328.6 3.6 fusion.66
  332.2 2.1 fusion.69
  334.3 0.1 pad_maximum_fusion
  334.4 0.0 copy-start.5
  334.4 1.4 copy.17
  335.8 0.0 reduce-scatter.4.cloned.1.call-update
  335.9 312.6 %reduce-scatter.4.cloned.1.call-done = bf16[16,1152]{1,0:T(8,128)(2,1)} async-done(((bf16[512,1152]{1,0:T(8,128)(2,1)}), bf16[16,1152]{1,0:T(8,128)(2,1)}) %reduce-scatter.4.cloned.1.call-update) | async-done | bytes 36880
  648.5 1.0 copy.18
  649.5 0.1 fusion.80
  649.6 0.7 copy.15
  650.4 0.7 copy.16
  (17 shorter events, 0.1 us)
Async XLA Ops:
  7.2 321.4 %all-reduce.3.cloned.1.call-start = ((), (), s32[]{:S(2)}) async-start(), calls=%async_computation.2 | async-start | bytes 4718592 | tf_op jit(solution)/shard_map/psum | solution.py:78
  13.0 3.8 copy-start
  13.1 106.5 %copy-start.3 = (bf16[576]{0:T(1024)(128)(2,1)S(1)}, bf16[576]{0:T(1024)(128)(2,1)}, u32[]{:S(2)}) copy-start(bf16[576]{0:T(1024)(128)(2,1)} %param.12) | copy-start | bytes 3460
  13.1 106.6 %copy-start.4 = (bf16[576]{0:T(1024)(128)(2,1)S(1)}, bf16[576]{0:T(1024)(128)(2,1)}, u32[]{:S(2)}) copy-start(bf16[576]{0:T(1024)(128)(2,1)} %param.13) | copy-start | bytes 3460
  126.3 1.3 copy-start.1
  126.4 522.1 %reduce-scatter.4.cloned.1.call-start = ((), (), s32[]{:S(2)}) async-start(), calls=%async_computation.1 | async-start | bytes 1216512
  127.7 1.8 copy-start.2
  328.6 3.6 copy-start.6
  334.4 1.4 copy-start.5
Sparse Core Ops, SparseCore 0:
  126.5 202.0 all-reduce.2
  336.0 312.4 reduce-scatter.3
where the time goes:
time: 658 us
  waiting for transfers between devices  512 us (78%)
  blocking collectives  102 us (16%)
  between operations  18.6 us (3%)
  matrix products  12.4 us (2%)
  local copies, waits for them, and re-layouts  7.57 us (1%)
    unnamed x3, waiting for transfers between devices  313 us
    psum x1, waiting for transfers between devices, body(): lax.psum(partial_minus.astype(jnp.bfloat16), 'tensor').astype(jnp.float32)  199 us
    psum x1, blocking collectives, body(): totals = lax.psum(jnp.sum(values, axis=1), 'tensor')  51.4 us
    psum x1, blocking collectives, body(): squares = lax.psum(jnp.sum(centered * centered, axis=1), 'tensor')  50.4 us
  transfers between devices with their start and end apart: 2, of which 2 were waited for; matrix products, arithmetic and copies ran while one was open for 0% of the time, Pallas kernels for 0%

commit v1 on v0

v1 whole, which is shorter than its diff:
```python
import jax
import jax.numpy as jnp
from jax import lax
from jax.sharding import Mesh, PartitionSpec as P

D = 9216
FF = 36864
TENSOR = ("zl", "c")
FSDP = ("y", "zh", "x")


def shift_xor(hashed, amount):
    return hashed ^ lax.shift_right_logical(hashed, jnp.int32(amount))


def hashed_noise(param_index, seed_value, hash_mults):
    mult_a = hash_mults[0] | 1
    mult_b = hash_mults[1] | 1
    mult_c = hash_mults[2] | 1
    hashed = param_index * mult_a + seed_value * mult_b
    hashed = shift_xor(hashed, 16)
    hashed = hashed * mult_c
    hashed = shift_xor(hashed, 13)
    hashed = hashed * mult_a
    hashed = shift_xor(hashed, 16)
    fraction = (hashed & 16777215).astype(jnp.float32) * (1.0 / 16777216.0)
    return (fraction - 0.5) * 3.4641016151377544


def new_weights(weight, param_index, update_step, perturb_scale, step_seeds, hash_mults):
    updated = (
        weight.astype(jnp.float32)
        - update_step[0] * hashed_noise(param_index, step_seeds[0], hash_mults)
    ).astype(jnp.bfloat16)
    updated = lax.optimization_barrier(updated)
    updated_f = updated.astype(jnp.float32)
    shift_term = perturb_scale[0] * hashed_noise(param_index, step_seeds[1], hash_mults)
    return (
        (updated_f + shift_term).astype(jnp.bfloat16),
        (updated_f - shift_term).astype(jnp.bfloat16),
    )


def line_perm(bit_of_core):
    return [(2 * z + c, 2 * (z ^ (1 << bit_of_core[c])) + c) for z in range(8) for c in range(2)]


STAGES = [(0, 1), (1, 0), (2, 2)]
CORE_SWAP = [(i, i ^ 1) for i in range(16)]


def total(value):
    value = value + lax.ppermute(value, TENSOR, CORE_SWAP)
    for bits in STAGES:
        value = value + lax.ppermute(value, TENSOR, line_perm(bits))
    return value


def half(array, which):
    rows = array.shape[0] // 2
    return lax.dynamic_slice_in_dim(array, which * rows, rows, 0)


def join(mine, other, which):
    return jnp.where(
        which == 0, jnp.concatenate([mine, other], 0), jnp.concatenate([other, mine], 0)
    )


def body(
    tokens,
    ln_gain,
    ln_bias,
    fc1_weight,
    fc1_bias,
    fc2_weight,
    fc2_bias,
    update_step,
    perturb_scale,
    step_seeds,
    hash_mults,
):
    bf16 = jnp.bfloat16
    f32 = jnp.float32
    feat_local = tokens.shape[1]
    unit_local = fc1_weight.shape[1]
    core = lax.axis_index("c")
    z_lo = lax.axis_index("zl")
    z_hi = lax.axis_index("zh")
    picks = [(core, CORE_SWAP)]
    for bits in STAGES:
        bit = jnp.where(core == 0, bits[0], bits[1])
        picks.append((lax.shift_right_logical(z_lo, bit) & 1, line_perm(bits)))

    values = tokens.astype(f32)
    row_mean = (total(jnp.sum(values, axis=1)) / D)[:, None]
    centered = values - row_mean
    row_var = (total(jnp.sum(centered * centered, axis=1)) / D)[:, None]
    normed = (
        centered * lax.rsqrt(row_var + 1e-05) * ln_gain.astype(f32) + ln_bias.astype(f32)
    ).astype(bf16)
    feat_ids = lax.axis_index(TENSOR) * feat_local + jnp.arange(feat_local, dtype=jnp.int32)
    unit_ids = lax.axis_index(FSDP) * unit_local + jnp.arange(unit_local, dtype=jnp.int32)
    first_index = feat_ids[:, None] * FF + unit_ids[None, :]
    plus_one, minus_one = new_weights(
        fc1_weight, first_index, update_step, perturb_scale, step_seeds, hash_mults
    )
    part = jnp.concatenate(
        [
            jnp.dot(normed, plus_one, preferred_element_type=f32).astype(bf16),
            jnp.dot(normed, minus_one, preferred_element_type=f32).astype(bf16),
        ],
        axis=1,
    )
    for which, perm in picks:
        other = lax.ppermute(half(part, 1 - which), TENSOR, perm)
        part = (half(part, which).astype(f32) + other.astype(f32)).astype(bf16)
    bias_one = fc1_bias.astype(f32)
    hidden = jax.nn.relu(part.astype(f32) + jnp.concatenate([bias_one, bias_one])).astype(bf16)
    for which, perm in picks[::-1]:
        hidden = join(hidden, lax.ppermute(hidden, TENSOR, perm), which)
    second_index = D * FF + unit_ids[:, None] * D + feat_ids[None, :]
    plus_two, minus_two = new_weights(
        fc2_weight, second_index, update_step, perturb_scale, step_seeds, hash_mults
    )
    out = jnp.concatenate(
        [
            jnp.dot(hidden[:, :unit_local], plus_two, preferred_element_type=f32),
            jnp.dot(hidden[:, unit_local:], minus_two, preferred_element_type=f32),
        ],
        axis=1,
    ).astype(bf16)
    width = 2 * feat_local
    out = out.reshape(4, 2, 4, -1, width).transpose(0, 2, 1, 3, 4).reshape(16, -1, width)
    out = lax.all_to_all(out, ("y", "x"), 0, 0, tiled=True)
    out = jnp.sum(out.astype(f32), axis=0)
    other = lax.ppermute(half(out, 1 - z_hi).astype(bf16), "zh", [(0, 1), (1, 0)])
    out = half(out, z_hi) + other.astype(f32)
    bias_two = fc2_bias.astype(f32)
    branch_plus = (out[:, :feat_local] + bias_two).astype(bf16)
    branch_minus = (out[:, feat_local:] + bias_two).astype(bf16)
    return (branch_plus, branch_minus)


def solution(mesh):
    fine = Mesh(mesh.devices.reshape(4, 2, 4, 8, 2), ("y", "zh", "x", "zl", "c"))
    in_specs = (
        P(None, TENSOR),
        P(TENSOR),
        P(TENSOR),
        P(TENSOR, FSDP),
        P(FSDP),
        P(FSDP, TENSOR),
        P(TENSOR),
        P(),
        P(),
        P(),
        P(),
    )
    out_specs = (P(FSDP, TENSOR), P(FSDP, TENSOR))
    return jax.shard_map(body, mesh=fine, in_specs=in_specs, out_specs=out_specs, check_vma=False)
```

time: 658 us -> 217 us (0.33)
  waiting for transfers between devices: 512 us -> 110 us
  blocking collectives: 102 us -> 0 us
  starting transfers between devices: 0.26 us -> 72.9 us
  between operations: 18.6 us -> 5.59 us
  other arithmetic: 5.64 us -> 12.7 us
    unnamed x3 -> x0, waiting for transfers between devices: 313 us -> none
    psum x1 -> x0, waiting for transfers between devices: 199 us -> none  [body(): lax.psum(partial_minus.astype(jnp.bfloat16), 'tensor').astype(jnp.float32)]
    psum x2 -> x0, blocking collectives: 102 us -> none  [the longest x1 51.4 us: body(): totals = lax.psum(jnp.sum(values, axis=1), 'tensor')]
    ppermute x0 -> x17, waiting for transfers between devices: none -> 92.4 us  [the longest x4 38.8 us: body(): other = lax.ppermute(half(part, 1 - which), TENSOR, perm)]
    ppermute x0 -> x17, starting transfers between devices: none -> 66.4 us  [the longest x6 18 us: total(): value = value + lax.ppermute(value, TENSOR, line_perm(bits))]
    all_to_all x0 -> x1, waiting for transfers between devices: none -> 17.9 us  [body(): out = lax.all_to_all(out, ('y', 'x'), 0, 0, tiled=True)]
  transfers between devices with their start and end apart: 2 -> 18, of which waited for: 2 -> 15; matrix products, arithmetic and copies ran while one was open for 0% -> 4% of each run, Pallas kernels for 0% -> 0%
where the time goes in v1:
time: 217 us; the launch traced here: 216 us
  waiting for transfers between devices  110 us (51%)
  starting transfers between devices  72.9 us (34%)
  other arithmetic  12.7 us (6%)
  matrix products  9.71 us (4%)
  between operations  5.59 us (3%)
  local copies, waits for them, and re-layouts  4.6 us (2%)
    ppermute x4, waiting for transfers between devices, body(): other = lax.ppermute(half(part, 1 - which), TENSOR, perm)  38.8 us
    ppermute x4, waiting for transfers between devices, body(): hidden = join(hidden, lax.ppermute(hidden, TENSOR, perm), which)  37.9 us
    ppermute x6, starting transfers between devices, total(): value = value + lax.ppermute(value, TENSOR, line_perm(bits))  18 us
    all_to_all x1, waiting for transfers between devices, body(): out = lax.all_to_all(out, ('y', 'x'), 0, 0, tiled=True)  17.9 us
    ppermute x2, starting transfers between devices, total(): value = value + lax.ppermute(value, TENSOR, CORE_SWAP)  14.5 us
    ppermute x4, starting transfers between devices, body(): other = lax.ppermute(half(part, 1 - which), TENSOR, perm)  13.9 us
    ppermute x6, waiting for transfers between devices, total(): value = value + lax.ppermute(value, TENSOR, line_perm(bits))  11.6 us
    ppermute x1, starting transfers between devices, body(): lax.ppermute(half(out, 1 - z_hi).astype(bf16), 'zh', [(0, 1), (1, 0)])  10.2 us
  transfers between devices with their start and end apart: 18, of which 15 were waited for; matrix products, arithmetic and copies ran while one was open for 4% of the time, Pallas kernels for 0%

profile of v1, /device:TPU:1, one launch (start us, length us, event | category | flops | bytes accessed | tf_op | source)
XLA Modules:
  0.0 215.8 jit_solution(6226529735932607336)
XLA Ops:
  1.9 8.8 %collective-permute-start = (f32[512]{0:T(512)S(1)}, f32[512]{0:T(512)S(1)}, u32[]{:S(2)}, u32[]{:S(2)}) collective-permute-start(f32[512]{0:T(512)S(1)} %convert_reduce_fusion.1), channel_id=1, source_target_pairs={{0,1},{1,0},{2,3},{3,2},{4,5},{5,4},{6,7},{7,6},{8,9},{9,8},{10,11... | collective-permute-start | bytes 6152 | tf_op jit(solution)/shard_map/ppermute | solution.py:53
  13.4 3.3 %collective-permute-done.1 = f32[512]{0:T(512)S(1)} collective-permute-done((f32[512]{0:T(512)S(1)}, f32[512]{0:T(512)S(1)}, u32[]{:S(2)}, u32[]{:S(2)}) %collective-permute-start.1) | collective-permute-done | bytes 2080 | tf_op jit(solution)/shard_map/ppermute | solution.py:55
  18.6 2.4 %collective-permute-done.2 = f32[512]{0:T(512)S(1)} collective-permute-done((f32[512]{0:T(512)S(1)}, f32[512]{0:T(512)S(1)}, u32[]{:S(2)}, u32[]{:S(2)}) %collective-permute-start.2) | collective-permute-done | bytes 2080 | tf_op jit(solution)/shard_map/ppermute | solution.py:55
  21.0 4.3 %collective-permute-start.3 = (f32[512]{0:T(512)S(1)}, f32[512]{0:T(512)S(1)}, u32[]{:S(2)}, u32[]{:S(2)}) collective-permute-start(f32[512]{0:T(512)S(1)} %add.216), channel_id=1, source_target_pairs={{0,8},{1,9},{2,10},{3,11},{4,12},{5,13},{6,14},{7,15},{8,0},{9,1},... | collective-permute-start | bytes 6152 | tf_op jit(solution)/shard_map/ppermute | solution.py:55
  25.3 3.9 %collective-permute-done.3 = f32[512]{0:T(512)S(1)} collective-permute-done((f32[512]{0:T(512)S(1)}, f32[512]{0:T(512)S(1)}, u32[]{:S(2)}, u32[]{:S(2)}) %collective-permute-start.3) | collective-permute-done | bytes 2080 | tf_op jit(solution)/shard_map/ppermute | solution.py:55
  30.5 5.7 %collective-permute-start.4 = (f32[512]{0:T(512)S(1)}, f32[512]{0:T(512)S(1)}, u32[]{:S(2)}, u32[]{:S(2)}) collective-permute-start(f32[512]{0:T(512)S(1)} %fusion.72), channel_id=1, source_target_pairs={{0,1},{1,0},{2,3},{3,2},{4,5},{5,4},{6,7},{7,6},{8,9},{9,8},{10,11... | collective-permute-start | bytes 6152 | tf_op jit(solution)/shard_map/ppermute | solution.py:53
  37.6 1.9 collective-permute-start.5
  40.9 2.0 collective-permute-done.5
  42.8 1.9 collective-permute-start.6
  47.9 6.1 %collective-permute-start.7 = (f32[512]{0:T(512)S(1)}, f32[512]{0:T(512)S(1)}, u32[]{:S(2)}, u32[]{:S(2)}) collective-permute-start(f32[512]{0:T(512)S(1)} %add.220), channel_id=1, source_target_pairs={{0,8},{1,9},{2,10},{3,11},{4,12},{5,13},{6,14},{7,15},{8,0},{9,1},... | collective-permute-start | bytes 6152 | tf_op jit(solution)/shard_map/ppermute | solution.py:55
  54.0 4.2 %fusion.35 = bf16[576,1152]{1,0:T(8,128)(2,1)} fusion(bf16[576,1152]{1,0:T(8,128)(2,1)} %param.14, f32[]{:T(128)} %bitcast.3, s32[]{:T(128)} %bitcast.2, s32[]{:T(128)} %bitcast.1, s32[]{:T(128)} %bitcast, s32[1152]{0:T(1024)S(1)} %iota_add_fusion, s32[576]{0:T(1024)S(1)} %broadcast_multiply_fusion), kind=kLoop, calls=%fused_computation.59 | loop fusion | flops 12607488 | bytes 2661136 | tf_op jit(solution)/shard_map/convert_element_type | solution.py:34
  59.6 3.7 %convolution_convert_fusion = bf16[512,1152]{1,0:T(8,128)(2,1)S(1)} fusion(bf16[576,1152]{1,0:T(8,128)(2,1)} %fusion.35, f32[]{:T(128)} %bitcast.5, s32[]{:T(128)} %bitcast.4, s32[]{:T(128)} %bitcast.2, s32[]{:T(128)} %bitcast, s32[1152]{0:T(1024)S(1)} %iota_add_fusion, s32[576]{0:T(1024)S(1)} %broadcast_multiply_fusion, bf16[512,576]{0,1:T(8,128)(2,1)S(1)} %copy-done, ...), kind=kOutput, calls=%fused_computation.16 | convolution fusion | flops 694444032 | bytes 3112208 | tf_op jit(solution)/shard_map/dot_general | solution.py:111
  63.3 2.3 %convolution_convert_fusion.1 = bf16[512,1152]{1,0:T(8,128)(2,1)S(1)} fusion(bf16[576,1152]{1,0:T(8,128)(2,1)S(1)} %copy-done.2, f32[]{:T(128)} %bitcast.5, s32[]{:T(128)} %bitcast.4, s32[]{:T(128)} %bitcast.2, s32[]{:T(128)} %bitcast, s32[1152]{0:T(1024)S(1)} %iota_add_fusion, s32[576]{0:T(1024)S(1)} %broadcast_multiply_fusion, ...), kind=kOutput, calls=%fused_computation.17 | convolution fusion | flops 694444032 | bytes 3112208 | tf_op jit(solution)/shard_map/dot_general | solution.py:110
  65.8 3.0 %collective-permute-start.8 = (bf16[256,2304]{1,0:T(8,128)(2,1)S(1)}, bf16[256,2304]{1,0:T(8,128)(2,1)}, u32[]{:S(2)}, u32[]{:S(2)}) collective-permute-start(bf16[256,2304]{1,0:T(8,128)(2,1)S(1)} %fusion.76), channel_id=1, source_target_pairs={{0,1},{1,0},{2,3},{3,2},{4,5},{5,4},{6,7},{7,6},{8,9},{9,8},{10,11... | collective-permute-start | bytes 3538952 | tf_op jit(solution)/shard_map/ppermute | solution.py:116
  68.9 2.6 %collective-permute-done.8 = bf16[256,2304]{1,0:T(8,128)(2,1)} collective-permute-done((bf16[256,2304]{1,0:T(8,128)(2,1)S(1)}, bf16[256,2304]{1,0:T(8,128)(2,1)}, u32[]{:S(2)}, u32[]{:S(2)}) %collective-permute-start.8) | collective-permute-done | bytes 1179680 | tf_op jit(solution)/shard_map/ppermute | solution.py:116
  73.0 3.1 %collective-permute-start.9 = (bf16[128,2304]{1,0:T(8,128)(2,1)S(1)}, bf16[128,2304]{1,0:T(8,128)(2,1)S(1)}, u32[]{:S(2)}, u32[]{:S(2)}) collective-permute-start(bf16[128,2304]{1,0:T(8,128)(2,1)S(1)} %constant_dynamic-slice_fusion.2), channel_id=1, source_target_pairs={{0,2},{1,5},{2,0},{3,7},{4,6},{5,1},{6,4},{7,3},{8,10},{9,13},{10,... | collective-permute-start | bytes 1769480 | tf_op jit(solution)/shard_map/ppermute | solution.py:116
  76.2 13.5 %collective-permute-done.9 = bf16[128,2304]{1,0:T(8,128)(2,1)S(1)} collective-permute-done((bf16[128,2304]{1,0:T(8,128)(2,1)S(1)}, bf16[128,2304]{1,0:T(8,128)(2,1)S(1)}, u32[]{:S(2)}, u32[]{:S(2)}) %collective-permute-start.9) | collective-permute-done | bytes 589856 | tf_op jit(solution)/shard_map/ppermute | solution.py:116
  89.8 4.1 %collective-permute-start.10 = (bf16[64,2304]{1,0:T(8,128)(2,1)S(1)}, bf16[64,2304]{1,0:T(8,128)(2,1)S(1)}, u32[]{:S(2)}, u32[]{:S(2)}) collective-permute-start(bf16[64,2304]{1,0:T(8,128)(2,1)S(1)} %constant_dynamic-slice_fusion.1), channel_id=1, source_target_pairs={{0,4},{1,3},{2,6},{3,1},{4,0},{5,7},{6,2},{7,5},{8,12},{9,11},{10,... | collective-permute-start | bytes 884744 | tf_op jit(solution)/shard_map/ppermute | solution.py:116
  93.9 6.4 %collective-permute-done.10 = bf16[64,2304]{1,0:T(8,128)(2,1)S(1)} collective-permute-done((bf16[64,2304]{1,0:T(8,128)(2,1)S(1)}, bf16[64,2304]{1,0:T(8,128)(2,1)S(1)}, u32[]{:S(2)}, u32[]{:S(2)}) %collective-permute-start.10) | collective-permute-done | bytes 294944 | tf_op jit(solution)/shard_map/ppermute | solution.py:116
  100.4 3.6 %collective-permute-start.11 = (bf16[32,2304]{1,0:T(8,128)(2,1)S(1)}, bf16[32,2304]{1,0:T(8,128)(2,1)S(1)}, u32[]{:S(2)}, u32[]{:S(2)}) collective-permute-start(bf16[32,2304]{1,0:T(8,128)(2,1)S(1)} %constant_dynamic-slice_fusion), channel_id=1, source_target_pairs={{0,8},{1,9},{2,10},{3,11},{4,12},{5,13},{6,14},{7,15},{8,0},{9,1},... | collective-permute-start | bytes 442376 | tf_op jit(solution)/shard_map/ppermute | solution.py:116
  104.1 16.4 %collective-permute-done.11 = bf16[32,2304]{1,0:T(8,128)(2,1)S(1)} collective-permute-done((bf16[32,2304]{1,0:T(8,128)(2,1)S(1)}, bf16[32,2304]{1,0:T(8,128)(2,1)S(1)}, u32[]{:S(2)}, u32[]{:S(2)}) %collective-permute-start.11) | collective-permute-done | bytes 147488 | tf_op jit(solution)/shard_map/ppermute | solution.py:116
  120.6 1.9 collective-permute-start.12
  122.5 15.0 %collective-permute-done.12 = bf16[32,2304]{1,0:T(8,128)(2,1)S(1)} collective-permute-done((bf16[32,2304]{1,0:T(8,128)(2,1)S(1)}, bf16[32,2304]{1,0:T(8,128)(2,1)S(1)}, u32[]{:S(2)}, u32[]{:S(2)}) %collective-permute-start.12) | collective-permute-done | bytes 147488 | tf_op jit(solution)/shard_map/ppermute | solution.py:121
  137.6 1.9 collective-permute-start.13
  139.5 6.5 %collective-permute-done.13 = bf16[64,2304]{1,0:T(8,128)(2,1)S(1)} collective-permute-done((bf16[64,2304]{1,0:T(8,128)(2,1)S(1)}, bf16[64,2304]{1,0:T(8,128)(2,1)S(1)}, u32[]{:S(2)}, u32[]{:S(2)}) %collective-permute-start.13) | collective-permute-done | bytes 294944 | tf_op jit(solution)/shard_map/ppermute | solution.py:121
  146.1 1.9 collective-permute-start.14
  148.0 16.0 %collective-permute-done.14 = bf16[128,2304]{1,0:T(8,128)(2,1)S(1)} collective-permute-done((bf16[128,2304]{1,0:T(8,128)(2,1)S(1)}, bf16[128,2304]{1,0:T(8,128)(2,1)S(1)}, u32[]{:S(2)}, u32[]{:S(2)}) %collective-permute-start.14) | collective-permute-done | bytes 589856 | tf_op jit(solution)/shard_map/ppermute | solution.py:121
  164.2 4.0 %collective-permute-start.15 = (bf16[256,2304]{1,0:T(8,128)(2,1)S(1)}, bf16[256,2304]{1,0:T(8,128)(2,1)S(1)}, u32[]{:S(2)}, u32[]{:S(2)}) collective-permute-start(bf16[256,2304]{1,0:T(8,128)(2,1)S(1)} %maximum_select_fusion.1), channel_id=1, source_target_pairs={{0,1},{1,0},{2,3},{3,2},{4,5},{5,4},{6,7},{7,6},{8,9},{9,8},{10,11... | collective-permute-start | bytes 3538952 | tf_op jit(solution)/shard_map/ppermute | solution.py:121
  176.9 6.5 %all-to-all-start = ((bf16[16,32,1152]{2,1,0:T(8,128)(2,1)}), bf16[16,32,1152]{2,1,0:T(8,128)(2,1)S(1)}, u32[]{:S(2)}, u32[]{:S(2)}) async-start(bf16[16,32,1152]{2,1,0:T(8,128)(2,1)} %bitcast.9), calls=%async_computation | async-start | bytes 2359296 | tf_op jit(solution)/shard_map/all_to_all | solution.py:135
  183.5 17.9 %all-to-all-done = bf16[16,32,1152]{2,1,0:T(8,128)(2,1)S(1)} async-done(((bf16[16,32,1152]{2,1,0:T(8,128)(2,1)}), bf16[16,32,1152]{2,1,0:T(8,128)(2,1)S(1)}, u32[]{:S(2)}, u32[]{:S(2)}) %all-to-all-start) | async-done | bytes 1179680 | tf_op jit(solution)/shard_map/all_to_all | solution.py:135
  201.6 10.2 %collective-permute-start.16 = (bf16[16,1152]{1,0:T(8,128)(2,1)S(1)}, bf16[16,1152]{1,0:T(8,128)(2,1)S(1)}, u32[]{:S(2)}, u32[]{:S(2)}) collective-permute-start(bf16[16,1152]{1,0:T(8,128)(2,1)S(1)} %dynamic-slice_convert_fusion), channel_id=1, source_target_pairs={{0,64},{64,0},{1,65},{65,1},{2,66},{66,2},{3,67},{67,3},{4,68},{68... | collective-permute-start | bytes 110600 | tf_op jit(solution)/shard_map/ppermute | solution.py:137
  211.8 3.3 %collective-permute-done.16 = bf16[16,1152]{1,0:T(8,128)(2,1)S(1)} collective-permute-done((bf16[16,1152]{1,0:T(8,128)(2,1)S(1)}, bf16[16,1152]{1,0:T(8,128)(2,1)S(1)}, u32[]{:S(2)}, u32[]{:S(2)}) %collective-permute-start.16) | collective-permute-done | bytes 36896 | tf_op jit(solution)/shard_map/ppermute | solution.py:137
  (64 shorter events, 21.8 us)
Async XLA Ops:
  0.6 59.0 %copy-start = (bf16[512,576]{0,1:T(8,128)(2,1)S(1)}, bf16[512,576]{0,1:T(8,128)(2,1)}, u32[]{:S(2)}) copy-start(bf16[512,576]{0,1:T(8,128)(2,1)} %param.11) | copy-start | bytes 1769476
  0.6 58.9 %copy-start.4 = (bf16[576]{0:T(1024)(128)(2,1)S(1)}, bf16[576]{0:T(1024)(128)(2,1)}, u32[]{:S(2)}) copy-start(bf16[576]{0:T(1024)(128)(2,1)} %param.12) | copy-start | bytes 3460
  0.7 58.9 %copy-start.5 = (bf16[576]{0:T(1024)(128)(2,1)S(1)}, bf16[576]{0:T(1024)(128)(2,1)}, u32[]{:S(2)}) copy-start(bf16[576]{0:T(1024)(128)(2,1)} %param.13) | copy-start | bytes 3460
  1.9 9.6 %collective-permute-start = (f32[512]{0:T(512)S(1)}, f32[512]{0:T(512)S(1)}, u32[]{:S(2)}, u32[]{:S(2)}) collective-permute-start(f32[512]{0:T(512)S(1)} %convert_reduce_fusion.1), channel_id=1, source_target_pairs={{0,1},{1,0},{2,3},{3,2},{4,5},{5,4},{6,7},{7,6},{8,9},{9,8},{10,11... | collective-permute-start | bytes 6152 | tf_op jit(solution)/shard_map/ppermute | solution.py:53
  11.5 5.2 %collective-permute-start.1 = (f32[512]{0:T(512)S(1)}, f32[512]{0:T(512)S(1)}, u32[]{:S(2)}, u32[]{:S(2)}) collective-permute-start(f32[512]{0:T(512)S(1)} %add.214), channel_id=1, source_target_pairs={{0,2},{1,5},{2,0},{3,7},{4,6},{5,1},{6,4},{7,3},{8,10},{9,13},{10,... | collective-permute-start | bytes 6152 | tf_op jit(solution)/shard_map/ppermute | solution.py:55
  16.7 4.3 %collective-permute-start.2 = (f32[512]{0:T(512)S(1)}, f32[512]{0:T(512)S(1)}, u32[]{:S(2)}, u32[]{:S(2)}) collective-permute-start(f32[512]{0:T(512)S(1)} %add.215), channel_id=1, source_target_pairs={{0,4},{1,3},{2,6},{3,1},{4,0},{5,7},{6,2},{7,5},{8,12},{9,11},{10,... | collective-permute-start | bytes 6152 | tf_op jit(solution)/shard_map/ppermute | solution.py:55
  21.0 8.2 %collective-permute-start.3 = (f32[512]{0:T(512)S(1)}, f32[512]{0:T(512)S(1)}, u32[]{:S(2)}, u32[]{:S(2)}) collective-permute-start(f32[512]{0:T(512)S(1)} %add.216), channel_id=1, source_target_pairs={{0,8},{1,9},{2,10},{3,11},{4,12},{5,13},{6,14},{7,15},{8,0},{9,1},... | collective-permute-start | bytes 6152 | tf_op jit(solution)/shard_map/ppermute | solution.py:55
  30.5 7.1 %collective-permute-start.4 = (f32[512]{0:T(512)S(1)}, f32[512]{0:T(512)S(1)}, u32[]{:S(2)}, u32[]{:S(2)}) collective-permute-start(f32[512]{0:T(512)S(1)} %fusion.72), channel_id=1, source_target_pairs={{0,1},{1,0},{2,3},{3,2},{4,5},{5,4},{6,7},{7,6},{8,9},{9,8},{10,11... | collective-permute-start | bytes 6152 | tf_op jit(solution)/shard_map/ppermute | solution.py:53
  37.6 5.2 %collective-permute-start.5 = (f32[512]{0:T(512)S(1)}, f32[512]{0:T(512)S(1)}, u32[]{:S(2)}, u32[]{:S(2)}) collective-permute-start(f32[512]{0:T(512)S(1)} %add.218), channel_id=1, source_target_pairs={{0,2},{1,5},{2,0},{3,7},{4,6},{5,1},{6,4},{7,3},{8,10},{9,13},{10,... | collective-permute-start | bytes 6152 | tf_op jit(solution)/shard_map/ppermute | solution.py:55
  42.8 5.1 %collective-permute-start.6 = (f32[512]{0:T(512)S(1)}, f32[512]{0:T(512)S(1)}, u32[]{:S(2)}, u32[]{:S(2)}) collective-permute-start(f32[512]{0:T(512)S(1)} %add.219), channel_id=1, source_target_pairs={{0,4},{1,3},{2,6},{3,1},{4,0},{5,7},{6,2},{7,5},{8,12},{9,11},{10,... | collective-permute-start | bytes 6152 | tf_op jit(solution)/shard_map/ppermute | solution.py:55
  47.9 11.7 %collective-permute-start.7 = (f32[512]{0:T(512)S(1)}, f32[512]{0:T(512)S(1)}, u32[]{:S(2)}, u32[]{:S(2)}) collective-permute-start(f32[512]{0:T(512)S(1)} %add.220), channel_id=1, source_target_pairs={{0,8},{1,9},{2,10},{3,11},{4,12},{5,13},{6,14},{7,15},{8,0},{9,1},... | collective-permute-start | bytes 6152 | tf_op jit(solution)/shard_map/ppermute | solution.py:55
  59.6 3.7 %copy-start.2 = (bf16[576,1152]{1,0:T(8,128)(2,1)S(1)}, bf16[576,1152]{1,0:T(8,128)(2,1)}, u32[]{:S(2)}) copy-start(bf16[576,1152]{1,0:T(8,128)(2,1)} %fusion.35) | copy-start | bytes 3981316
  65.8 5.6 %collective-permute-start.8 = (bf16[256,2304]{1,0:T(8,128)(2,1)S(1)}, bf16[256,2304]{1,0:T(8,128)(2,1)}, u32[]{:S(2)}, u32[]{:S(2)}) collective-permute-start(bf16[256,2304]{1,0:T(8,128)(2,1)S(1)} %fusion.76), channel_id=1, source_target_pairs={{0,1},{1,0},{2,3},{3,2},{4,5},{5,4},{6,7},{7,6},{8,9},{9,8},{10,11... | collective-permute-start | bytes 3538952 | tf_op jit(solution)/shard_map/ppermute | solution.py:116
  73.0 31.1 %copy-start.3 = (bf16[1152]{0:T(1024)(128)(2,1)S(1)}, bf16[1152]{0:T(1024)(128)(2,1)}, u32[]{:S(2)}) copy-start(bf16[1152]{0:T(1024)(128)(2,1)} %param.15) | copy-start | bytes 6916
  73.0 16.6 %collective-permute-start.9 = (bf16[128,2304]{1,0:T(8,128)(2,1)S(1)}, bf16[128,2304]{1,0:T(8,128)(2,1)S(1)}, u32[]{:S(2)}, u32[]{:S(2)}) collective-permute-start(bf16[128,2304]{1,0:T(8,128)(2,1)S(1)} %constant_dynamic-slice_fusion.2), channel_id=1, source_target_pairs={{0,2},{1,5},{2,0},{3,7},{4,6},{5,1},{6,4},{7,3},{8,10},{9,13},{10,... | collective-permute-start | bytes 1769480 | tf_op jit(solution)/shard_map/ppermute | solution.py:116
  89.8 10.5 %collective-permute-start.10 = (bf16[64,2304]{1,0:T(8,128)(2,1)S(1)}, bf16[64,2304]{1,0:T(8,128)(2,1)S(1)}, u32[]{:S(2)}, u32[]{:S(2)}) collective-permute-start(bf16[64,2304]{1,0:T(8,128)(2,1)S(1)} %constant_dynamic-slice_fusion.1), channel_id=1, source_target_pairs={{0,4},{1,3},{2,6},{3,1},{4,0},{5,7},{6,2},{7,5},{8,12},{9,11},{10,... | collective-permute-start | bytes 884744 | tf_op jit(solution)/shard_map/ppermute | solution.py:116
  100.4 67.9 %copy-start.1 = (bf16[1152,576]{0,1:T(8,128)(2,1)S(1)}, bf16[1152,576]{0,1:T(8,128)(2,1)}, u32[]{:S(2)}) copy-start(bf16[1152,576]{0,1:T(8,128)(2,1)} %param.16) | copy-start | bytes 3981316
  100.4 20.1 %collective-permute-start.11 = (bf16[32,2304]{1,0:T(8,128)(2,1)S(1)}, bf16[32,2304]{1,0:T(8,128)(2,1)S(1)}, u32[]{:S(2)}, u32[]{:S(2)}) collective-permute-start(bf16[32,2304]{1,0:T(8,128)(2,1)S(1)} %constant_dynamic-slice_fusion), channel_id=1, source_target_pairs={{0,8},{1,9},{2,10},{3,11},{4,12},{5,13},{6,14},{7,15},{8,0},{9,1},... | collective-permute-start | bytes 442376 | tf_op jit(solution)/shard_map/ppermute | solution.py:116
  120.6 17.0 %collective-permute-start.12 = (bf16[32,2304]{1,0:T(8,128)(2,1)S(1)}, bf16[32,2304]{1,0:T(8,128)(2,1)S(1)}, u32[]{:S(2)}, u32[]{:S(2)}) collective-permute-start(bf16[32,2304]{1,0:T(8,128)(2,1)S(1)} %maximum_convert_fusion), channel_id=1, source_target_pairs={{0,8},{1,9},{2,10},{3,11},{4,12},{5,13},{6,14},{7,15},{8,0},{9,1},... | collective-permute-start | bytes 442376 | tf_op jit(solution)/shard_map/ppermute | solution.py:121
  137.6 8.4 %collective-permute-start.13 = (bf16[64,2304]{1,0:T(8,128)(2,1)S(1)}, bf16[64,2304]{1,0:T(8,128)(2,1)S(1)}, u32[]{:S(2)}, u32[]{:S(2)}) collective-permute-start(bf16[64,2304]{1,0:T(8,128)(2,1)S(1)} %maximum_select_fusion.3), channel_id=1, source_target_pairs={{0,4},{1,3},{2,6},{3,1},{4,0},{5,7},{6,2},{7,5},{8,12},{9,11},{10,... | collective-permute-start | bytes 884744 | tf_op jit(solution)/shard_map/ppermute | solution.py:121
  146.1 18.0 %collective-permute-start.14 = (bf16[128,2304]{1,0:T(8,128)(2,1)S(1)}, bf16[128,2304]{1,0:T(8,128)(2,1)S(1)}, u32[]{:S(2)}, u32[]{:S(2)}) collective-permute-start(bf16[128,2304]{1,0:T(8,128)(2,1)S(1)} %maximum_select_fusion.2), channel_id=1, source_target_pairs={{0,2},{1,5},{2,0},{3,7},{4,6},{5,1},{6,4},{7,3},{8,10},{9,13},{10,... | collective-permute-start | bytes 1769480 | tf_op jit(solution)/shard_map/ppermute | solution.py:121
  164.2 6.3 %collective-permute-start.15 = (bf16[256,2304]{1,0:T(8,128)(2,1)S(1)}, bf16[256,2304]{1,0:T(8,128)(2,1)S(1)}, u32[]{:S(2)}, u32[]{:S(2)}) collective-permute-start(bf16[256,2304]{1,0:T(8,128)(2,1)S(1)} %maximum_select_fusion.1), channel_id=1, source_target_pairs={{0,1},{1,0},{2,3},{3,2},{4,5},{5,4},{6,7},{7,6},{8,9},{9,8},{10,11... | collective-permute-start | bytes 3538952 | tf_op jit(solution)/shard_map/ppermute | solution.py:121
  176.9 34.9 %copy-start.6 = (bf16[576]{0:T(1024)(128)(2,1)S(1)}, bf16[576]{0:T(1024)(128)(2,1)}, u32[]{:S(2)}) copy-start(bf16[576]{0:T(1024)(128)(2,1)} %param.17) | copy-start | bytes 3460
  176.9 24.4 %all-to-all-start = ((bf16[16,32,1152]{2,1,0:T(8,128)(2,1)}), bf16[16,32,1152]{2,1,0:T(8,128)(2,1)S(1)}, u32[]{:S(2)}, u32[]{:S(2)}) async-start(bf16[16,32,1152]{2,1,0:T(8,128)(2,1)} %bitcast.9), calls=%async_computation | async-start | bytes 2359296 | tf_op jit(solution)/shard_map/all_to_all | solution.py:135
  201.6 13.5 %collective-permute-start.16 = (bf16[16,1152]{1,0:T(8,128)(2,1)S(1)}, bf16[16,1152]{1,0:T(8,128)(2,1)S(1)}, u32[]{:S(2)}, u32[]{:S(2)}) collective-permute-start(bf16[16,1152]{1,0:T(8,128)(2,1)S(1)} %dynamic-slice_convert_fusion), channel_id=1, source_target_pairs={{0,64},{64,0},{1,65},{65,1},{2,66},{66,2},{3,67},{67,3},{4,68},{68... | collective-permute-start | bytes 110600 | tf_op jit(solution)/shard_map/ppermute | solution.py:137

commit v2 on v1

--- a/solution.py
+++ b/solution.py
@@ -49,13 +49,6 @@
 CORE_SWAP = [(i, i ^ 1) for i in range(16)]
 
 
-def total(value):
-    value = value + lax.ppermute(value, TENSOR, CORE_SWAP)
-    for bits in STAGES:
-        value = value + lax.ppermute(value, TENSOR, line_perm(bits))
-    return value
-
-
 def half(array, which):
     rows = array.shape[0] // 2
     return lax.dynamic_slice_in_dim(array, which * rows, rows, 0)
@@ -93,9 +86,16 @@
         picks.append((lax.shift_right_logical(z_lo, bit) & 1, line_perm(bits)))
 
     values = tokens.astype(f32)
-    row_mean = (total(jnp.sum(values, axis=1)) / D)[:, None]
-    centered = values - row_mean
-    row_var = (total(jnp.sum(centered * centered, axis=1)) / D)[:, None]
+    local_mean = jnp.mean(values, axis=1)
+    offset = values - local_mean[:, None]
+    local_sq = jnp.sum(offset * offset, axis=1)
+    stats = jnp.broadcast_to(jnp.stack([local_mean, local_sq])[None], (16, 2, tokens.shape[0]))
+    stats = lax.all_to_all(stats, TENSOR, 0, 0, tiled=True)
+    means = stats[:, 0]
+    row_mean = jnp.mean(means, axis=0)
+    spread = means - row_mean[None]
+    row_var = (jnp.sum(stats[:, 1] + feat_local * spread * spread, axis=0) / D)[:, None]
+    centered = values - row_mean[:, None]
     normed = (
         centered * lax.rsqrt(row_var + 1e-05) * ln_gain.astype(f32) + ln_bias.astype(f32)
     ).astype(bf16)
@@ -105,41 +105,36 @@
     plus_one, minus_one = new_weights(
         fc1_weight, first_index, update_step, perturb_scale, step_seeds, hash_mults
     )
-    part = jnp.concatenate(
-        [
-            jnp.dot(normed, plus_one, preferred_element_type=f32).astype(bf16),
-            jnp.dot(normed, minus_one, preferred_element_type=f32).astype(bf16),
-        ],
-        axis=1,
+    plus_two, minus_two = new_weights(
+        fc2_weight,
+        D * FF + unit_ids[:, None] * D + feat_ids[None, :],
+        update_step,
+        perturb_scale,
+        step_seeds,
+        hash_mults,
     )
-    for which, perm in picks:
-        other = lax.ppermute(half(part, 1 - which), TENSOR, perm)
-        part = (half(part, which).astype(f32) + other.astype(f32)).astype(bf16)
     bias_one = fc1_bias.astype(f32)
-    hidden = jax.nn.relu(part.astype(f32) + jnp.concatenate([bias_one, bias_one])).astype(bf16)
-    for which, perm in picks[::-1]:
-        hidden = join(hidden, lax.ppermute(hidden, TENSOR, perm), which)
-    second_index = D * FF + unit_ids[:, None] * D + feat_ids[None, :]
-    plus_two, minus_two = new_weights(
-        fc2_weight, second_index, update_step, perturb_scale, step_seeds, hash_mults
-    )
-    out = jnp.concatenate(
-        [
-            jnp.dot(hidden[:, :unit_local], plus_two, preferred_element_type=f32),
-            jnp.dot(hidden[:, unit_local:], minus_two, preferred_element_type=f32),
-        ],
-        axis=1,
-    ).astype(bf16)
-    width = 2 * feat_local
-    out = out.reshape(4, 2, 4, -1, width).transpose(0, 2, 1, 3, 4).reshape(16, -1, width)
-    out = lax.all_to_all(out, ("y", "x"), 0, 0, tiled=True)
-    out = jnp.sum(out.astype(f32), axis=0)
-    other = lax.ppermute(half(out, 1 - z_hi).astype(bf16), "zh", [(0, 1), (1, 0)])
-    out = half(out, z_hi) + other.astype(f32)
     bias_two = fc2_bias.astype(f32)
-    branch_plus = (out[:, :feat_local] + bias_two).astype(bf16)
-    branch_minus = (out[:, feat_local:] + bias_two).astype(bf16)
-    return (branch_plus, branch_minus)
+    hidden = []
+    for weight in (plus_one, minus_one):
+        part = jnp.dot(normed, weight, preferred_element_type=f32).astype(bf16)
+        for which, perm in picks:
+            other = lax.ppermute(half(part, 1 - which), TENSOR, perm)
+            part = (half(part, which).astype(f32) + other.astype(f32)).astype(bf16)
+        hidden.append(jax.nn.relu(part.astype(f32) + bias_one).astype(bf16))
+    for stage in range(len(picks)):
+        which, perm = picks[-1 - stage]
+        hidden = [join(one, lax.ppermute(one, TENSOR, perm), which) for one in hidden]
+    results = []
+    for one, weight in zip(hidden, (plus_two, minus_two)):
+        out = jnp.dot(one, weight, preferred_element_type=f32).astype(bf16)
+        out = out.reshape(4, 2, 4, -1, feat_local).transpose(0, 2, 1, 3, 4)
+        out = out.reshape(16, -1, feat_local)
+        out = lax.all_to_all(out, ("y", "x"), 0, 0, tiled=True)
+        out = jnp.sum(out.astype(f32), axis=0)
+        other = lax.ppermute(half(out, 1 - z_hi).astype(bf16), "zh", [(0, 1), (1, 0)])
+        results.append((half(out, z_hi) + other.astype(f32) + bias_two).astype(bf16))
+    return tuple(results)
 
 
 def solution(mesh):

time: 217 us -> 180 us (0.83)
  waiting for transfers between devices: 110 us -> 58 us
  starting transfers between devices: 72.9 us -> 90.9 us
  other arithmetic: 12.7 us -> 8.22 us
    ppermute x12 -> x8, waiting for transfers between devices: 50.3 us -> 17.2 us  [body(): lax.ppermute(one, TENSOR, perm)]
    ppermute x4 -> x8, waiting for transfers between devices: 38.8 us -> 22 us  [body(): other = lax.ppermute(half(part, 1 - which), TENSOR, perm)]
    ppermute x12 -> x8, starting transfers between devices: 42.3 us -> 26.4 us  [body(): lax.ppermute(one, TENSOR, perm)]
    all_to_all x0 -> x1, starting transfers between devices: none -> 14 us  [body(): stats = lax.all_to_all(stats, TENSOR, 0, 0, tiled=True)]
    ppermute x4 -> x8, starting transfers between devices: 13.9 us -> 24 us  [body(): other = lax.ppermute(half(part, 1 - which), TENSOR, perm)]
    all_to_all x1 -> x2, waiting for transfers between devices: 17.9 us -> 11.4 us  [body(): out = lax.all_to_all(out, ('y', 'x'), 0, 0, tiled=True)]
    ppermute x1 -> x2, starting transfers between devices: 10.2 us -> 16 us  [body(): lax.ppermute(half(out, 1 - z_hi).astype(bf16), 'zh', [(0, 1), (1, 0)])]
    all_to_all x1 -> x2, starting transfers between devices: 6.5 us -> 10.4 us  [body(): out = lax.all_to_all(out, ('y', 'x'), 0, 0, tiled=True)]
  transfers between devices with their start and end apart: 18 -> 21, of which waited for: 15 -> 14; matrix products, arithmetic and copies ran while one was open for 4% -> 9% of each run, Pallas kernels for 0% -> 0%
where the time goes in v2:
time: 180 us; the launch traced here: 178 us
  starting transfers between devices  90.9 us (50%)
  waiting for transfers between devices  58 us (32%)
  matrix products  9.96 us (6%)
  other arithmetic  8.22 us (5%)
  between operations  5.84 us (3%)
  local copies, waits for them, and re-layouts  4.63 us (3%)
    ppermute x8, starting transfers between devices, body(): lax.ppermute(one, TENSOR, perm)  26.4 us
    ppermute x8, starting transfers between devices, body(): other = lax.ppermute(half(part, 1 - which), TENSOR, perm)  24 us
    ppermute x8, waiting for transfers between devices, body(): other = lax.ppermute(half(part, 1 - which), TENSOR, perm)  22 us
    ppermute x8, waiting for transfers between devices, body(): lax.ppermute(one, TENSOR, perm)  17.2 us
    ppermute x2, starting transfers between devices, body(): lax.ppermute(half(out, 1 - z_hi).astype(bf16), 'zh', [(0, 1), (1, 0)])  16 us
    all_to_all x1, starting transfers between devices, body(): stats = lax.all_to_all(stats, TENSOR, 0, 0, tiled=True)  14 us
    all_to_all x2, waiting for transfers between devices, body(): out = lax.all_to_all(out, ('y', 'x'), 0, 0, tiled=True)  11.4 us
    all_to_all x2, starting transfers between devices, body(): out = lax.all_to_all(out, ('y', 'x'), 0, 0, tiled=True)  10.4 us
  transfers between devices with their start and end apart: 21, of which 14 were waited for; matrix products, arithmetic and copies ran while one was open for 9% of the time, Pallas kernels for 0%

profile of v2, /device:TPU:1, one launch (start us, length us, event | category | flops | bytes accessed | tf_op | source)
XLA Modules:
  0.0 177.6 jit_solution(8233369694401515799)
XLA Ops:
  3.9 14.0 %all-to-all-start = ((f32[16,2,512]{2,1,0:T(2,128)}), f32[16,2,512]{2,1,0:T(2,128)S(1)}, u32[]{:S(2)}, u32[]{:S(2)}) async-start(f32[16,2,512]{2,1,0:T(2,128)} %broadcast_in_dim.2), calls=%async_computation | async-start | bytes 131072 | tf_op jit(solution)/shard_map/all_to_all | solution.py:93
  25.7 2.3 %all-to-all-done = f32[16,2,512]{2,1,0:T(2,128)S(1)} async-done(((f32[16,2,512]{2,1,0:T(2,128)}), f32[16,2,512]{2,1,0:T(2,128)S(1)}, u32[]{:S(2)}, u32[]{:S(2)}) %all-to-all-start) | async-done | bytes 65568 | tf_op jit(solution)/shard_map/all_to_all | solution.py:93
  28.1 2.3 %convolution_convert_fusion.1 = bf16[512,1152]{1,0:T(8,128)(2,1)S(1)} fusion(bf16[576,1152]{1,0:T(8,128)(2,1)S(1)} %fusion.35, f32[]{:T(128)} %bitcast.8, s32[]{:T(128)} %bitcast.7, s32[]{:T(128)} %bitcast.5, s32[]{:T(128)} %bitcast.3, s32[1152]{0:T(1024)S(1)} %iota_add_fusion, s32[576]{0:T(1024)S(1)} %broadcast_multiply_fusion, ...), kind=kOutput, calls=%fused_computation.17 | convolution fusion | flops 694444032 | bytes 3112208 | tf_op jit(solution)/shard_map/dot_general | solution.py:120
  30.5 2.9 %collective-permute-start = (bf16[256,1152]{1,0:T(8,128)(2,1)S(1)}, bf16[256,1152]{1,0:T(8,128)(2,1)S(1)}, u32[]{:S(2)}, u32[]{:S(2)}) collective-permute-start(bf16[256,1152]{1,0:T(8,128)(2,1)S(1)} %constant_dynamic-slice_fusion.7), channel_id=1, source_target_pairs={{0,1},{1,0},{2,3},{3,2},{4,5},{5,4},{6,7},{7,6},{8,9},{9,8},{10,11... | collective-permute-start | bytes 1769480 | tf_op jit(solution)/shard_map/ppermute | solution.py:122
  33.4 2.3 %convolution_convert_fusion = bf16[512,1152]{1,0:T(8,128)(2,1)S(1)} fusion(bf16[576,1152]{1,0:T(8,128)(2,1)S(1)} %fusion.35, f32[]{:T(128)} %bitcast.8, s32[]{:T(128)} %bitcast.7, s32[]{:T(128)} %bitcast.5, s32[]{:T(128)} %bitcast.3, s32[1152]{0:T(1024)S(1)} %iota_add_fusion, s32[576]{0:T(1024)S(1)} %broadcast_multiply_fusion, ...), kind=kOutput, calls=%fused_computation.16 | convolution fusion | flops 694444032 | bytes 3112208 | tf_op jit(solution)/shard_map/dot_general | solution.py:120
  35.8 1.9 %collective-permute-start.9 = (bf16[256,1152]{1,0:T(8,128)(2,1)S(1)}, bf16[256,1152]{1,0:T(8,128)(2,1)S(1)}, u32[]{:S(2)}, u32[]{:S(2)}) collective-permute-start(bf16[256,1152]{1,0:T(8,128)(2,1)S(1)} %constant_dynamic-slice_fusion.3), channel_id=1, source_target_pairs={{0,1},{1,0},{2,3},{3,2},{4,5},{5,4},{6,7},{7,6},{8,9},{9,8},{10,11... | collective-permute-start | bytes 1769480 | tf_op jit(solution)/shard_map/ppermute | solution.py:122
  38.0 1.9 %collective-permute-start.1 = (bf16[128,1152]{1,0:T(8,128)(2,1)S(1)}, bf16[128,1152]{1,0:T(8,128)(2,1)S(1)}, u32[]{:S(2)}, u32[]{:S(2)}) collective-permute-start(bf16[128,1152]{1,0:T(8,128)(2,1)S(1)} %constant_dynamic-slice_fusion.6), channel_id=1, source_target_pairs={{0,2},{1,5},{2,0},{3,7},{4,6},{5,1},{6,4},{7,3},{8,10},{9,13},{10,... | collective-permute-start | bytes 884744 | tf_op jit(solution)/shard_map/ppermute | solution.py:122
  40.1 4.3 %collective-permute-start.10 = (bf16[128,1152]{1,0:T(8,128)(2,1)S(1)}, bf16[128,1152]{1,0:T(8,128)(2,1)S(1)}, u32[]{:S(2)}, u32[]{:S(2)}) collective-permute-start(bf16[128,1152]{1,0:T(8,128)(2,1)S(1)} %constant_dynamic-slice_fusion.2), channel_id=1, source_target_pairs={{0,2},{1,5},{2,0},{3,7},{4,6},{5,1},{6,4},{7,3},{8,10},{9,13},{10,... | collective-permute-start | bytes 884744 | tf_op jit(solution)/shard_map/ppermute | solution.py:122
  44.4 5.1 %collective-permute-done.1 = bf16[128,1152]{1,0:T(8,128)(2,1)S(1)} collective-permute-done((bf16[128,1152]{1,0:T(8,128)(2,1)S(1)}, bf16[128,1152]{1,0:T(8,128)(2,1)S(1)}, u32[]{:S(2)}, u32[]{:S(2)}) %collective-permute-start.1) | collective-permute-done | bytes 294944 | tf_op jit(solution)/shard_map/ppermute | solution.py:122
  51.5 4.1 %collective-permute-done.10 = bf16[128,1152]{1,0:T(8,128)(2,1)S(1)} collective-permute-done((bf16[128,1152]{1,0:T(8,128)(2,1)S(1)}, bf16[128,1152]{1,0:T(8,128)(2,1)S(1)}, u32[]{:S(2)}, u32[]{:S(2)}) %collective-permute-start.10) | collective-permute-done | bytes 294944 | tf_op jit(solution)/shard_map/ppermute | solution.py:122
  55.8 1.9 %collective-permute-start.11 = (bf16[64,1152]{1,0:T(8,128)(2,1)S(1)}, bf16[64,1152]{1,0:T(8,128)(2,1)S(1)}, u32[]{:S(2)}, u32[]{:S(2)}) collective-permute-start(bf16[64,1152]{1,0:T(8,128)(2,1)S(1)} %constant_dynamic-slice_fusion.1), channel_id=1, source_target_pairs={{0,4},{1,3},{2,6},{3,1},{4,0},{5,7},{6,2},{7,5},{8,12},{9,11},{10,... | collective-permute-start | bytes 442376 | tf_op jit(solution)/shard_map/ppermute | solution.py:122
  59.3 4.2 %collective-permute-start.3 = (bf16[32,1152]{1,0:T(8,128)(2,1)S(1)}, bf16[32,1152]{1,0:T(8,128)(2,1)S(1)}, u32[]{:S(2)}, u32[]{:S(2)}) collective-permute-start(bf16[32,1152]{1,0:T(8,128)(2,1)S(1)} %constant_dynamic-slice_fusion.4), channel_id=1, source_target_pairs={{0,8},{1,9},{2,10},{3,11},{4,12},{5,13},{6,14},{7,15},{8,0},{9,1},... | collective-permute-start | bytes 221192 | tf_op jit(solution)/shard_map/ppermute | solution.py:122
  63.5 5.0 %collective-permute-start.12 = (bf16[32,1152]{1,0:T(8,128)(2,1)S(1)}, bf16[32,1152]{1,0:T(8,128)(2,1)S(1)}, u32[]{:S(2)}, u32[]{:S(2)}) collective-permute-start(bf16[32,1152]{1,0:T(8,128)(2,1)S(1)} %constant_dynamic-slice_fusion), channel_id=1, source_target_pairs={{0,8},{1,9},{2,10},{3,11},{4,12},{5,13},{6,14},{7,15},{8,0},{9,1},... | collective-permute-start | bytes 221192 | tf_op jit(solution)/shard_map/ppermute | solution.py:122
  68.6 3.5 %collective-permute-done.3 = bf16[32,1152]{1,0:T(8,128)(2,1)S(1)} collective-permute-done((bf16[32,1152]{1,0:T(8,128)(2,1)S(1)}, bf16[32,1152]{1,0:T(8,128)(2,1)S(1)}, u32[]{:S(2)}, u32[]{:S(2)}) %collective-permute-start.3) | collective-permute-done | bytes 73760 | tf_op jit(solution)/shard_map/ppermute | solution.py:122
  72.1 7.8 %collective-permute-done.12 = bf16[32,1152]{1,0:T(8,128)(2,1)S(1)} collective-permute-done((bf16[32,1152]{1,0:T(8,128)(2,1)S(1)}, bf16[32,1152]{1,0:T(8,128)(2,1)S(1)}, u32[]{:S(2)}, u32[]{:S(2)}) %collective-permute-start.12) | collective-permute-done | bytes 73760 | tf_op jit(solution)/shard_map/ppermute | solution.py:122
  81.9 7.3 %collective-permute-start.13 = (bf16[32,1152]{1,0:T(8,128)(2,1)S(1)}, bf16[32,1152]{1,0:T(8,128)(2,1)S(1)}, u32[]{:S(2)}, u32[]{:S(2)}) collective-permute-start(bf16[32,1152]{1,0:T(8,128)(2,1)S(1)} %get-tuple-element.5), channel_id=1, source_target_pairs={{0,8},{1,9},{2,10},{3,11},{4,12},{5,13},{6,14},{7,15},{8,0},{9,1},... | collective-permute-start | bytes 221192 | tf_op jit(solution)/shard_map/ppermute | solution.py:127
  89.1 7.1 %collective-permute-done.4 = bf16[32,1152]{1,0:T(8,128)(2,1)S(1)} collective-permute-done((bf16[32,1152]{1,0:T(8,128)(2,1)S(1)}, bf16[32,1152]{1,0:T(8,128)(2,1)S(1)}, u32[]{:S(2)}, u32[]{:S(2)}) %collective-permute-start.4) | collective-permute-done | bytes 73760 | tf_op jit(solution)/shard_map/ppermute | solution.py:127
  96.3 2.1 %collective-permute-start.5 = (bf16[64,1152]{1,0:T(8,128)(2,1)S(1)}, bf16[64,1152]{1,0:T(8,128)(2,1)S(1)}, u32[]{:S(2)}, u32[]{:S(2)}) collective-permute-start(bf16[64,1152]{1,0:T(8,128)(2,1)S(1)} %maximum_select_fusion.8), channel_id=1, source_target_pairs={{0,4},{1,3},{2,6},{3,1},{4,0},{5,7},{6,2},{7,5},{8,12},{9,11},{10,... | collective-permute-start | bytes 442376 | tf_op jit(solution)/shard_map/ppermute | solution.py:127
  98.7 3.1 %collective-permute-start.14 = (bf16[64,1152]{1,0:T(8,128)(2,1)S(1)}, bf16[64,1152]{1,0:T(8,128)(2,1)S(1)}, u32[]{:S(2)}, u32[]{:S(2)}) collective-permute-start(bf16[64,1152]{1,0:T(8,128)(2,1)S(1)} %maximum_select_fusion.9), channel_id=1, source_target_pairs={{0,4},{1,3},{2,6},{3,1},{4,0},{5,7},{6,2},{7,5},{8,12},{9,11},{10,... | collective-permute-start | bytes 442376 | tf_op jit(solution)/shard_map/ppermute | solution.py:127
  104.3 3.5 %collective-permute-done.14 = bf16[64,1152]{1,0:T(8,128)(2,1)S(1)} collective-permute-done((bf16[64,1152]{1,0:T(8,128)(2,1)S(1)}, bf16[64,1152]{1,0:T(8,128)(2,1)S(1)}, u32[]{:S(2)}, u32[]{:S(2)}) %collective-permute-start.14) | collective-permute-done | bytes 147488 | tf_op jit(solution)/shard_map/ppermute | solution.py:127
  109.8 5.7 %collective-permute-done.6 = bf16[128,1152]{1,0:T(8,128)(2,1)S(1)} collective-permute-done((bf16[128,1152]{1,0:T(8,128)(2,1)S(1)}, bf16[128,1152]{1,0:T(8,128)(2,1)S(1)}, u32[]{:S(2)}, u32[]{:S(2)}) %collective-permute-start.6) | collective-permute-done | bytes 294944 | tf_op jit(solution)/shard_map/ppermute | solution.py:127
  115.7 4.2 %collective-permute-start.7 = (bf16[256,1152]{1,0:T(8,128)(2,1)S(1)}, bf16[256,1152]{1,0:T(8,128)(2,1)S(1)}, u32[]{:S(2)}, u32[]{:S(2)}) collective-permute-start(bf16[256,1152]{1,0:T(8,128)(2,1)S(1)} %maximum_select_fusion.4), channel_id=1, source_target_pairs={{0,1},{1,0},{2,3},{3,2},{4,5},{5,4},{6,7},{7,6},{8,9},{9,8},{10,11... | collective-permute-start | bytes 1769480 | tf_op jit(solution)/shard_map/ppermute | solution.py:127
  121.9 4.0 %collective-permute-start.16 = (bf16[256,1152]{1,0:T(8,128)(2,1)S(1)}, bf16[256,1152]{1,0:T(8,128)(2,1)}, u32[]{:S(2)}, u32[]{:S(2)}) collective-permute-start(bf16[256,1152]{1,0:T(8,128)(2,1)S(1)} %maximum_select_fusion.5), channel_id=1, source_target_pairs={{0,1},{1,0},{2,3},{3,2},{4,5},{5,4},{6,7},{7,6},{8,9},{9,8},{10,11... | collective-permute-start | bytes 1769480 | tf_op jit(solution)/shard_map/ppermute | solution.py:127
  125.9 2.0 %fusion.64 = bf16[512,576]{0,1:T(8,128)(2,1)S(1)} fusion(bf16[1152,576]{0,1:T(8,128)(2,1)S(1)} %fusion.34, f32[]{:T(128)} %bitcast.8, s32[]{:T(128)} %bitcast.7, s32[]{:T(128)} %bitcast.5, s32[]{:T(128)} %bitcast.3, s32[576]{0:T(1024)S(1)} %iota_add_fusion.1, s32[1152]{0:T(1024)S(1)} %multiply_add_fusion, bf16[256,1152]{1,0:T(8,128)(2,1)S(1)} %collective-permute-done.7, ...), kind=kOutput, calls=%fused_computation.83 | convolution fusion | flops 697688064 | bytes 3103505 | tf_op jit(solution)/shard_map/dot_general | solution.py:130
  129.1 6.7 %all-to-all-start.1 = ((bf16[16,32,576]{2,1,0:T(8,128)(2,1)}), bf16[16,32,576]{2,1,0:T(8,128)(2,1)S(1)}, u32[]{:S(2)}, u32[]{:S(2)}) async-start(bf16[16,32,576]{2,1,0:T(8,128)(2,1)} %bitcast.11), calls=%async_computation.1 | async-start | bytes 1310720 | tf_op jit(solution)/shard_map/all_to_all | solution.py:133
  135.8 3.3 %fusion.67 = bf16[512,576]{0,1:T(8,128)(2,1)S(1)} fusion(bf16[1152,576]{0,1:T(8,128)(2,1)S(1)} %fusion.34, f32[]{:T(128)} %bitcast.8, s32[]{:T(128)} %bitcast.7, s32[]{:T(128)} %bitcast.5, s32[]{:T(128)} %bitcast.3, s32[576]{0:T(1024)S(1)} %iota_add_fusion.1, s32[1152]{0:T(1024)S(1)} %multiply_add_fusion, bf16[256,1152]{1,0:T(8,128)(2,1)} %collective-permute-done.16, ...), kind=kOutput, calls=%fused_computation.84 | convolution fusion | flops 697688064 | bytes 3103505 | tf_op jit(solution)/shard_map/dot_general | solution.py:130
  140.3 8.0 %all-to-all-done.1 = bf16[16,32,576]{2,1,0:T(8,128)(2,1)S(1)} async-done(((bf16[16,32,576]{2,1,0:T(8,128)(2,1)}), bf16[16,32,576]{2,1,0:T(8,128)(2,1)S(1)}, u32[]{:S(2)}, u32[]{:S(2)}) %all-to-all-start.1) | async-done | bytes 589856 | tf_op jit(solution)/shard_map/all_to_all | solution.py:133
  148.3 3.7 %all-to-all-start.2 = ((bf16[16,32,576]{2,1,0:T(8,128)(2,1)}), bf16[16,32,576]{2,1,0:T(8,128)(2,1)S(1)}, u32[]{:S(2)}, u32[]{:S(2)}) async-start(bf16[16,32,576]{2,1,0:T(8,128)(2,1)} %bitcast.14), calls=%async_computation.2 | async-start | bytes 1310720 | tf_op jit(solution)/shard_map/all_to_all | solution.py:133
  152.1 8.0 %collective-permute-start.8 = (bf16[16,576]{1,0:T(8,128)(2,1)S(1)}, bf16[16,576]{1,0:T(8,128)(2,1)S(1)}, u32[]{:S(2)}, u32[]{:S(2)}) collective-permute-start(bf16[16,576]{1,0:T(8,128)(2,1)S(1)} %dynamic-slice_convert_fusion.1), channel_id=1, source_target_pairs={{0,64},{64,0},{1,65},{65,1},{2,66},{66,2},{3,67},{67,3},{4,68},{68... | collective-permute-start | bytes 55304 | tf_op jit(solution)/shard_map/ppermute | solution.py:135
  160.1 3.4 %all-to-all-done.2 = bf16[16,32,576]{2,1,0:T(8,128)(2,1)S(1)} async-done(((bf16[16,32,576]{2,1,0:T(8,128)(2,1)}), bf16[16,32,576]{2,1,0:T(8,128)(2,1)S(1)}, u32[]{:S(2)}, u32[]{:S(2)}) %all-to-all-start.2) | async-done | bytes 589856 | tf_op jit(solution)/shard_map/all_to_all | solution.py:133
  163.7 8.0 %collective-permute-start.17 = (bf16[16,576]{1,0:T(8,128)(2,1)S(1)}, bf16[16,576]{1,0:T(8,128)(2,1)S(1)}, u32[]{:S(2)}, u32[]{:S(2)}) collective-permute-start(bf16[16,576]{1,0:T(8,128)(2,1)S(1)} %dynamic-slice_convert_fusion), channel_id=1, source_target_pairs={{0,64},{64,0},{1,65},{65,1},{2,66},{66,2},{3,67},{67,3},{4,68},{68... | collective-permute-start | bytes 55304 | tf_op jit(solution)/shard_map/ppermute | solution.py:135
  171.7 5.2 %collective-permute-done.17 = bf16[16,576]{1,0:T(8,128)(2,1)S(1)} collective-permute-done((bf16[16,576]{1,0:T(8,128)(2,1)S(1)}, bf16[16,576]{1,0:T(8,128)(2,1)S(1)}, u32[]{:S(2)}, u32[]{:S(2)}) %collective-permute-start.17) | collective-permute-done | bytes 18464 | tf_op jit(solution)/shard_map/ppermute | solution.py:135
  (83 shorter events, 22.9 us)
Async XLA Ops:
  0.6 17.3 %copy-start.3 = (s32[3]{0:T(128)S(1)}, s32[3]{0:T(128)}, u32[]{:S(2)}) copy-start(s32[3]{0:T(128)} %param.21) | copy-start | bytes 40
  0.6 19.8 %copy-start.8 = (s32[2]{0:T(128)S(1)}, s32[2]{0:T(128)}, u32[]{:S(2)}) copy-start(s32[2]{0:T(128)} %param.20) | copy-start | bytes 28
  0.7 21.8 %copy-start.1 = (bf16[576,1152]{1,0:T(8,128)(2,1)S(1)}, bf16[576,1152]{1,0:T(8,128)(2,1)}, u32[]{:S(2)}) copy-start(bf16[576,1152]{1,0:T(8,128)(2,1)} %param.14) | copy-start | bytes 3981316
  3.9 24.1 %all-to-all-start = ((f32[16,2,512]{2,1,0:T(2,128)}), f32[16,2,512]{2,1,0:T(2,128)S(1)}, u32[]{:S(2)}, u32[]{:S(2)}) async-start(f32[16,2,512]{2,1,0:T(2,128)} %broadcast_in_dim.2), calls=%async_computation | async-start | bytes 131072 | tf_op jit(solution)/shard_map/all_to_all | solution.py:93
  22.5 3.2 %copy-start.5 = (bf16[576]{0:T(1024)(128)(2,1)S(1)}, bf16[576]{0:T(1024)(128)(2,1)}, u32[]{:S(2)}) copy-start(bf16[576]{0:T(1024)(128)(2,1)} %param.12) | copy-start | bytes 3460
  22.5 3.2 %copy-start.6 = (bf16[576]{0:T(1024)(128)(2,1)S(1)}, bf16[576]{0:T(1024)(128)(2,1)}, u32[]{:S(2)}) copy-start(bf16[576]{0:T(1024)(128)(2,1)} %param.13) | copy-start | bytes 3460
  22.5 5.6 %copy-start = (bf16[512,576]{0,1:T(8,128)(2,1)S(1)}, bf16[512,576]{0,1:T(8,128)(2,1)}, u32[]{:S(2)}) copy-start(bf16[512,576]{0,1:T(8,128)(2,1)} %param.11) | copy-start | bytes 1769476
  30.5 7.2 %collective-permute-start = (bf16[256,1152]{1,0:T(8,128)(2,1)S(1)}, bf16[256,1152]{1,0:T(8,128)(2,1)S(1)}, u32[]{:S(2)}, u32[]{:S(2)}) collective-permute-start(bf16[256,1152]{1,0:T(8,128)(2,1)S(1)} %constant_dynamic-slice_fusion.7), channel_id=1, source_target_pairs={{0,1},{1,0},{2,3},{3,2},{4,5},{5,4},{6,7},{7,6},{8,9},{9,8},{10,11... | collective-permute-start | bytes 1769480 | tf_op jit(solution)/shard_map/ppermute | solution.py:122
  35.8 4.1 %collective-permute-start.9 = (bf16[256,1152]{1,0:T(8,128)(2,1)S(1)}, bf16[256,1152]{1,0:T(8,128)(2,1)S(1)}, u32[]{:S(2)}, u32[]{:S(2)}) collective-permute-start(bf16[256,1152]{1,0:T(8,128)(2,1)S(1)} %constant_dynamic-slice_fusion.3), channel_id=1, source_target_pairs={{0,1},{1,0},{2,3},{3,2},{4,5},{5,4},{6,7},{7,6},{8,9},{9,8},{10,11... | collective-permute-start | bytes 1769480 | tf_op jit(solution)/shard_map/ppermute | solution.py:122
  38.0 11.5 %collective-permute-start.1 = (bf16[128,1152]{1,0:T(8,128)(2,1)S(1)}, bf16[128,1152]{1,0:T(8,128)(2,1)S(1)}, u32[]{:S(2)}, u32[]{:S(2)}) collective-permute-start(bf16[128,1152]{1,0:T(8,128)(2,1)S(1)} %constant_dynamic-slice_fusion.6), channel_id=1, source_target_pairs={{0,2},{1,5},{2,0},{3,7},{4,6},{5,1},{6,4},{7,3},{8,10},{9,13},{10,... | collective-permute-start | bytes 884744 | tf_op jit(solution)/shard_map/ppermute | solution.py:122
  40.1 15.6 %collective-permute-start.10 = (bf16[128,1152]{1,0:T(8,128)(2,1)S(1)}, bf16[128,1152]{1,0:T(8,128)(2,1)S(1)}, u32[]{:S(2)}, u32[]{:S(2)}) collective-permute-start(bf16[128,1152]{1,0:T(8,128)(2,1)S(1)} %constant_dynamic-slice_fusion.2), channel_id=1, source_target_pairs={{0,2},{1,5},{2,0},{3,7},{4,6},{5,1},{6,4},{7,3},{8,10},{9,13},{10,... | collective-permute-start | bytes 884744 | tf_op jit(solution)/shard_map/ppermute | solution.py:122
  49.6 19.0 %copy-start.4 = (bf16[1152]{0:T(1024)(128)(2,1)S(1)}, bf16[1152]{0:T(1024)(128)(2,1)}, u32[]{:S(2)}) copy-start(bf16[1152]{0:T(1024)(128)(2,1)} %param.15) | copy-start | bytes 6916
  49.6 9.6 %collective-permute-start.2 = (bf16[64,1152]{1,0:T(8,128)(2,1)S(1)}, bf16[64,1152]{1,0:T(8,128)(2,1)S(1)}, u32[]{:S(2)}, u32[]{:S(2)}) collective-permute-start(bf16[64,1152]{1,0:T(8,128)(2,1)S(1)} %constant_dynamic-slice_fusion.5), channel_id=1, source_target_pairs={{0,4},{1,3},{2,6},{3,1},{4,0},{5,7},{6,2},{7,5},{8,12},{9,11},{10,... | collective-permute-start | bytes 442376 | tf_op jit(solution)/shard_map/ppermute | solution.py:122
  55.8 7.7 %collective-permute-start.11 = (bf16[64,1152]{1,0:T(8,128)(2,1)S(1)}, bf16[64,1152]{1,0:T(8,128)(2,1)S(1)}, u32[]{:S(2)}, u32[]{:S(2)}) collective-permute-start(bf16[64,1152]{1,0:T(8,128)(2,1)S(1)} %constant_dynamic-slice_fusion.1), channel_id=1, source_target_pairs={{0,4},{1,3},{2,6},{3,1},{4,0},{5,7},{6,2},{7,5},{8,12},{9,11},{10,... | collective-permute-start | bytes 442376 | tf_op jit(solution)/shard_map/ppermute | solution.py:122
  59.3 12.8 %collective-permute-start.3 = (bf16[32,1152]{1,0:T(8,128)(2,1)S(1)}, bf16[32,1152]{1,0:T(8,128)(2,1)S(1)}, u32[]{:S(2)}, u32[]{:S(2)}) collective-permute-start(bf16[32,1152]{1,0:T(8,128)(2,1)S(1)} %constant_dynamic-slice_fusion.4), channel_id=1, source_target_pairs={{0,8},{1,9},{2,10},{3,11},{4,12},{5,13},{6,14},{7,15},{8,0},{9,1},... | collective-permute-start | bytes 221192 | tf_op jit(solution)/shard_map/ppermute | solution.py:122
  63.5 16.3 %collective-permute-start.12 = (bf16[32,1152]{1,0:T(8,128)(2,1)S(1)}, bf16[32,1152]{1,0:T(8,128)(2,1)S(1)}, u32[]{:S(2)}, u32[]{:S(2)}) collective-permute-start(bf16[32,1152]{1,0:T(8,128)(2,1)S(1)} %constant_dynamic-slice_fusion), channel_id=1, source_target_pairs={{0,8},{1,9},{2,10},{3,11},{4,12},{5,13},{6,14},{7,15},{8,0},{9,1},... | collective-permute-start | bytes 221192 | tf_op jit(solution)/shard_map/ppermute | solution.py:122
  79.9 16.3 %collective-permute-start.4 = (bf16[32,1152]{1,0:T(8,128)(2,1)S(1)}, bf16[32,1152]{1,0:T(8,128)(2,1)S(1)}, u32[]{:S(2)}, u32[]{:S(2)}) collective-permute-start(bf16[32,1152]{1,0:T(8,128)(2,1)S(1)} %get-tuple-element.6), channel_id=1, source_target_pairs={{0,8},{1,9},{2,10},{3,11},{4,12},{5,13},{6,14},{7,15},{8,0},{9,1},... | collective-permute-start | bytes 221192 | tf_op jit(solution)/shard_map/ppermute | solution.py:127
  81.9 16.8 %collective-permute-start.13 = (bf16[32,1152]{1,0:T(8,128)(2,1)S(1)}, bf16[32,1152]{1,0:T(8,128)(2,1)S(1)}, u32[]{:S(2)}, u32[]{:S(2)}) collective-permute-start(bf16[32,1152]{1,0:T(8,128)(2,1)S(1)} %get-tuple-element.5), channel_id=1, source_target_pairs={{0,8},{1,9},{2,10},{3,11},{4,12},{5,13},{6,14},{7,15},{8,0},{9,1},... | collective-permute-start | bytes 221192 | tf_op jit(solution)/shard_map/ppermute | solution.py:127
  96.3 23.6 %copy-start.2 = (bf16[1152,576]{0,1:T(8,128)(2,1)S(1)}, bf16[1152,576]{0,1:T(8,128)(2,1)}, u32[]{:S(2)}) copy-start(bf16[1152,576]{0,1:T(8,128)(2,1)} %param.16) | copy-start | bytes 3981316
  96.3 6.0 %collective-permute-start.5 = (bf16[64,1152]{1,0:T(8,128)(2,1)S(1)}, bf16[64,1152]{1,0:T(8,128)(2,1)S(1)}, u32[]{:S(2)}, u32[]{:S(2)}) collective-permute-start(bf16[64,1152]{1,0:T(8,128)(2,1)S(1)} %maximum_select_fusion.8), channel_id=1, source_target_pairs={{0,4},{1,3},{2,6},{3,1},{4,0},{5,7},{6,2},{7,5},{8,12},{9,11},{10,... | collective-permute-start | bytes 442376 | tf_op jit(solution)/shard_map/ppermute | solution.py:127
  98.7 9.2 %collective-permute-start.14 = (bf16[64,1152]{1,0:T(8,128)(2,1)S(1)}, bf16[64,1152]{1,0:T(8,128)(2,1)S(1)}, u32[]{:S(2)}, u32[]{:S(2)}) collective-permute-start(bf16[64,1152]{1,0:T(8,128)(2,1)S(1)} %maximum_select_fusion.9), channel_id=1, source_target_pairs={{0,4},{1,3},{2,6},{3,1},{4,0},{5,7},{6,2},{7,5},{8,12},{9,11},{10,... | collective-permute-start | bytes 442376 | tf_op jit(solution)/shard_map/ppermute | solution.py:127
  102.4 13.2 %collective-permute-start.6 = (bf16[128,1152]{1,0:T(8,128)(2,1)S(1)}, bf16[128,1152]{1,0:T(8,128)(2,1)S(1)}, u32[]{:S(2)}, u32[]{:S(2)}) collective-permute-start(bf16[128,1152]{1,0:T(8,128)(2,1)S(1)} %maximum_select_fusion.6), channel_id=1, source_target_pairs={{0,2},{1,5},{2,0},{3,7},{4,6},{5,1},{6,4},{7,3},{8,10},{9,13},{10,... | collective-permute-start | bytes 884744 | tf_op jit(solution)/shard_map/ppermute | solution.py:127
  107.9 13.8 %collective-permute-start.15 = (bf16[128,1152]{1,0:T(8,128)(2,1)S(1)}, bf16[128,1152]{1,0:T(8,128)(2,1)S(1)}, u32[]{:S(2)}, u32[]{:S(2)}) collective-permute-start(bf16[128,1152]{1,0:T(8,128)(2,1)S(1)} %maximum_select_fusion.7), channel_id=1, source_target_pairs={{0,2},{1,5},{2,0},{3,7},{4,6},{5,1},{6,4},{7,3},{8,10},{9,13},{10,... | collective-permute-start | bytes 884744 | tf_op jit(solution)/shard_map/ppermute | solution.py:127
  115.7 10.2 %collective-permute-start.7 = (bf16[256,1152]{1,0:T(8,128)(2,1)S(1)}, bf16[256,1152]{1,0:T(8,128)(2,1)S(1)}, u32[]{:S(2)}, u32[]{:S(2)}) collective-permute-start(bf16[256,1152]{1,0:T(8,128)(2,1)S(1)} %maximum_select_fusion.4), channel_id=1, source_target_pairs={{0,1},{1,0},{2,3},{3,2},{4,5},{5,4},{6,7},{7,6},{8,9},{9,8},{10,11... | collective-permute-start | bytes 1769480 | tf_op jit(solution)/shard_map/ppermute | solution.py:127
  121.9 13.9 %collective-permute-start.16 = (bf16[256,1152]{1,0:T(8,128)(2,1)S(1)}, bf16[256,1152]{1,0:T(8,128)(2,1)}, u32[]{:S(2)}, u32[]{:S(2)}) collective-permute-start(bf16[256,1152]{1,0:T(8,128)(2,1)S(1)} %maximum_select_fusion.5), channel_id=1, source_target_pairs={{0,1},{1,0},{2,3},{3,2},{4,5},{5,4},{6,7},{7,6},{8,9},{9,8},{10,11... | collective-permute-start | bytes 1769480 | tf_op jit(solution)/shard_map/ppermute | solution.py:127
  129.1 19.2 %all-to-all-start.1 = ((bf16[16,32,576]{2,1,0:T(8,128)(2,1)}), bf16[16,32,576]{2,1,0:T(8,128)(2,1)S(1)}, u32[]{:S(2)}, u32[]{:S(2)}) async-start(bf16[16,32,576]{2,1,0:T(8,128)(2,1)} %bitcast.11), calls=%async_computation.1 | async-start | bytes 1310720 | tf_op jit(solution)/shard_map/all_to_all | solution.py:133
  148.3 23.4 %copy-start.7 = (bf16[576]{0:T(1024)(128)(2,1)S(1)}, bf16[576]{0:T(1024)(128)(2,1)}, u32[]{:S(2)}) copy-start(bf16[576]{0:T(1024)(128)(2,1)} %param.17) | copy-start | bytes 3460
  148.3 15.3 %all-to-all-start.2 = ((bf16[16,32,576]{2,1,0:T(8,128)(2,1)}), bf16[16,32,576]{2,1,0:T(8,128)(2,1)S(1)}, u32[]{:S(2)}, u32[]{:S(2)}) async-start(bf16[16,32,576]{2,1,0:T(8,128)(2,1)} %bitcast.14), calls=%async_computation.2 | async-start | bytes 1310720 | tf_op jit(solution)/shard_map/all_to_all | solution.py:133
  152.1 19.6 %collective-permute-start.8 = (bf16[16,576]{1,0:T(8,128)(2,1)S(1)}, bf16[16,576]{1,0:T(8,128)(2,1)S(1)}, u32[]{:S(2)}, u32[]{:S(2)}) collective-permute-start(bf16[16,576]{1,0:T(8,128)(2,1)S(1)} %dynamic-slice_convert_fusion.1), channel_id=1, source_target_pairs={{0,64},{64,0},{1,65},{65,1},{2,66},{66,2},{3,67},{67,3},{4,68},{68... | collective-permute-start | bytes 55304 | tf_op jit(solution)/shard_map/ppermute | solution.py:135
  163.7 13.2 %collective-permute-start.17 = (bf16[16,576]{1,0:T(8,128)(2,1)S(1)}, bf16[16,576]{1,0:T(8,128)(2,1)S(1)}, u32[]{:S(2)}, u32[]{:S(2)}) collective-permute-start(bf16[16,576]{1,0:T(8,128)(2,1)S(1)} %dynamic-slice_convert_fusion), channel_id=1, source_target_pairs={{0,64},{64,0},{1,65},{65,1},{2,66},{66,2},{3,67},{67,3},{4,68},{68... | collective-permute-start | bytes 55304 | tf_op jit(solution)/shard_map/ppermute | solution.py:135

commit v3 on v2

v3 whole, which is shorter than its diff:
```python
import jax
import jax.numpy as jnp
from jax import lax
from jax.experimental import pallas as pl
from jax.experimental.pallas import tpu as pltpu
from jax.sharding import Mesh, PartitionSpec as P

D = 9216
FF = 36864
TENSOR = ("zl", "c")
FSDP = ("y", "zh", "x")


def shift_xor(hashed, amount):
    return hashed ^ lax.shift_right_logical(hashed, jnp.int32(amount))


def perturb_kernel(first, strides, block, strip, row_axes, col_axes):
    stride, col_stride = strides
    row_names, row_count = row_axes
    col_names, col_count = col_axes

    def kernel(seeds, mults, step, scale, weight, plus, minus):
        mult_a = mults[0] | 1
        mult_b = mults[1] | 1
        mult_c = mults[2] | 1
        unit = 3.4641016151377544 / 16777216.0
        step_unit = step[0] * unit
        scale_unit = scale[0] * unit
        columns = weight.shape[1]
        row_start = flat_index(row_names) * row_count + pl.program_id(0) * block
        start = first + row_start * stride + flat_index(col_names) * (col_count * col_stride)
        shape = (strip, columns)
        local = lax.broadcasted_iota(jnp.int32, shape, 0) * stride
        local = (local + lax.broadcasted_iota(jnp.int32, shape, 1) * col_stride) * mult_a

        def centred(hashed):
            hashed = shift_xor(hashed, 16)
            hashed = hashed * mult_c
            hashed = shift_xor(hashed, 13)
            hashed = hashed * mult_a
            hashed = shift_xor(hashed, 16)
            return ((hashed & 16777215) - 8388608).astype(jnp.float32)

        def body(index, carry):
            rows = pl.ds(index * strip, strip)
            base = (start + index * (strip * stride)) * mult_a
            noise = centred(local + (base + seeds[0] * mult_b))
            updated = (weight[rows, :].astype(jnp.float32) - step_unit * noise).astype(jnp.bfloat16)
            updated = updated.astype(jnp.float32)
            shift = scale_unit * centred(local + (base + seeds[1] * mult_b))
            plus[rows, :] = (updated + shift).astype(jnp.bfloat16)
            minus[rows, :] = (updated - shift).astype(jnp.bfloat16)
            return carry

        lax.fori_loop(0, block // strip, body, 0)

    return kernel


AXES = {"y": 4, "zh": 2, "x": 4, "zl": 8, "c": 2}


def flat_index(names):
    index = 0
    for name in names:
        index = index * AXES[name] + lax.axis_index(name)
    return index


def perturbed(weight, first, strides, row_names, col_names, scalars, steps):
    rows, columns = weight.shape
    block = rows // steps
    small = pl.BlockSpec(memory_space=pltpu.SMEM)
    tile = pl.BlockSpec((block, columns), lambda i: (i, 0))
    shape = jax.ShapeDtypeStruct((rows, columns), jnp.bfloat16)
    return pl.pallas_call(
        perturb_kernel(
            first, strides, block, 16, (row_names, rows), (col_names, columns)
        ),
        grid=(steps,),
        in_specs=[small] * 4 + [tile],
        out_specs=[tile, tile],
        out_shape=[shape, shape],
    )(*scalars, weight)


def line_perm(bit_of_core):
    return [(2 * z + c, 2 * (z ^ (1 << bit_of_core[c])) + c) for z in range(8) for c in range(2)]


STAGES = [(0, 1), (1, 0), (2, 2)]
CORE_SWAP = [(i, i ^ 1) for i in range(16)]


def after(value, earlier):
    return lax.optimization_barrier((value, earlier))[0]


def half(array, which):
    rows = array.shape[0] // 2
    return lax.dynamic_slice_in_dim(array, which * rows, rows, 0)


def join(mine, other, which):
    return jnp.where(
        which == 0, jnp.concatenate([mine, other], 0), jnp.concatenate([other, mine], 0)
    )


def body(
    tokens,
    ln_gain,
    ln_bias,
    fc1_weight,
    fc1_bias,
    fc2_weight,
    fc2_bias,
    update_step,
    perturb_scale,
    step_seeds,
    hash_mults,
):
    bf16 = jnp.bfloat16
    f32 = jnp.float32
    feat_local = tokens.shape[1]
    unit_local = fc1_weight.shape[1]
    core = lax.axis_index("c")
    z_lo = lax.axis_index("zl")
    z_hi = lax.axis_index("zh")
    picks = [(core, CORE_SWAP)]
    for bits in STAGES:
        bit = jnp.where(core == 0, bits[0], bits[1])
        picks.append((lax.shift_right_logical(z_lo, bit) & 1, line_perm(bits)))

    values = tokens.astype(f32)
    local_mean = jnp.mean(values, axis=1)
    offset = values - local_mean[:, None]
    local_sq = jnp.sum(offset * offset, axis=1)
    stats = jnp.broadcast_to(jnp.stack([local_mean, local_sq])[None], (16, 2, tokens.shape[0]))
    stats = lax.all_to_all(stats, TENSOR, 0, 0, tiled=True)
    scaled = (offset * ln_gain.astype(f32)).astype(bf16)
    slot = lax.broadcasted_iota(jnp.int32, (8, feat_local), 0)
    pair = jnp.where(slot == core, ln_gain[None], 0) + jnp.where(slot == 2, ln_bias[None], 0)
    pair = pair.astype(bf16)

    scalars = (step_seeds, hash_mults, update_step, perturb_scale)
    first_weights = perturbed(fc1_weight, 0, (FF, 1), TENSOR, FSDP, scalars, 4)
    second_weights = perturbed(fc2_weight.T, D * FF, (1, D), TENSOR, FSDP, scalars, 4)
    bias_one = fc1_bias.astype(f32)
    bias_two = fc2_bias.astype(f32)

    parts = [jnp.dot(scaled, w, preferred_element_type=f32).astype(bf16) for w in first_weights]
    sides = jnp.concatenate(
        [jnp.dot(pair, w, preferred_element_type=f32) for w in first_weights], axis=1
    )

    which, perm = picks[0]
    others = [lax.ppermute(half(part, 1 - which), TENSOR, perm) for part in parts]
    sides = sides + lax.ppermute(sides, TENSOR, perm)
    parts = [
        (half(part, which).astype(f32) + other.astype(f32)).astype(bf16)
        for part, other in zip(parts, others)
    ]

    which, perm = picks[1]
    rows = tokens.shape[0] // 4
    stats = lax.dynamic_slice_in_dim(stats, core * 2 * rows + which * rows, rows, 2)
    means = stats[:, 0]
    row_mean = jnp.mean(means, axis=0)
    spread = means - row_mean[None]
    row_var = jnp.sum(stats[:, 1] + feat_local * spread * spread, axis=0) / D
    row_scale = lax.rsqrt(row_var + 1e-05)[:, None]
    far = z_lo ^ jnp.where(core == 0, 1 << STAGES[0][0], 1 << STAGES[0][1])
    chips = lax.broadcasted_iota(jnp.int32, (16, rows), 0)
    near_rows = jnp.where(lax.shift_right_logical(chips, 1) == z_lo, spread, 0)
    far_rows = jnp.where(lax.shift_right_logical(chips, 1) == far, spread, 0)
    fold = lambda one: jnp.sum(one.reshape(8, 2, rows), axis=0)
    gap = jnp.zeros((6, rows), f32)
    spread = jnp.concatenate([fold(near_rows), gap, fold(far_rows), gap], axis=0)

    others = [lax.ppermute(half(part, 1 - which), TENSOR, perm) for part in parts]
    far_sides = lax.ppermute(sides, TENSOR, perm)
    both = jnp.concatenate([sides, far_sides], axis=0)
    shift = lax.dot_general(
        spread, both, (((0,), (0,)), ((), ())), precision=lax.Precision.HIGHEST
    )
    bias_sum = both[2:3] + both[10:11]
    for sign in range(2):
        columns = slice(sign * unit_local, (sign + 1) * unit_local)
        part = half(parts[sign], which).astype(f32) + others[sign].astype(f32)
        parts[sign] = (row_scale * (part + shift[:, columns]) + bias_sum[:, columns]).astype(bf16)

    hidden = []
    for part in parts:
        for which, perm in picks[2:]:
            other = lax.ppermute(half(part, 1 - which), TENSOR, perm)
            part = (half(part, which).astype(f32) + other.astype(f32)).astype(bf16)
        if hidden:
            part = after(part, hidden[0])
        hidden.append(jax.nn.relu(part.astype(f32) + bias_one).astype(bf16))
    for which, perm in picks[::-1]:
        hidden = [join(one, lax.ppermute(one, TENSOR, perm), which) for one in hidden]
    out = jnp.concatenate(
        [
            jnp.dot(one, weight.T, preferred_element_type=f32).astype(bf16)
            for one, weight in zip(hidden, second_weights)
        ],
        axis=1,
    )
    width = 2 * feat_local
    out = out.reshape(4, 2, 4, -1, width).transpose(0, 2, 1, 3, 4).reshape(16, -1, width)
    out = lax.all_to_all(out, ("y", "x"), 0, 0, tiled=True)
    out = jnp.sum(out.astype(f32), axis=0)
    other = lax.ppermute(half(out, 1 - z_hi).astype(bf16), "zh", [(0, 1), (1, 0)])
    out = half(out, z_hi) + other.astype(f32)
    branch_plus = (out[:, :feat_local] + bias_two).astype(bf16)
    branch_minus = (out[:, feat_local:] + bias_two).astype(bf16)
    return (branch_plus, branch_minus)


def solution(mesh):
    fine = Mesh(mesh.devices.reshape(4, 2, 4, 8, 2), ("y", "zh", "x", "zl", "c"))
    in_specs = (
        P(None, TENSOR),
        P(TENSOR),
        P(TENSOR),
        P(TENSOR, FSDP),
        P(FSDP),
        P(FSDP, TENSOR),
        P(TENSOR),
        P(),
        P(),
        P(),
        P(),
    )
    out_specs = (P(FSDP, TENSOR), P(FSDP, TENSOR))
    return jax.shard_map(body, mesh=fine, in_specs=in_specs, out_specs=out_specs, check_vma=False)
```

time: 180 us -> 196 us (1.089)
  Pallas kernels: 0 us -> 11.3 us
  starting transfers between devices: 90.9 us -> 99.4 us
  between operations: 5.84 us -> 2.6 us
    ppermute x8 -> x4, waiting for transfers between devices: 22 us -> 3.22 us  [body(): other = lax.ppermute(half(part, 1 - which), TENSOR, perm)]
    ppermute x0 -> x6, starting transfers between devices: none -> 17.6 us  [the longest x4 11.1 us: body(): lax.ppermute(half(part, 1 - which), TENSOR, perm)]
    ppermute x0 -> x6, waiting for transfers between devices: none -> 11.6 us  [the longest x4 9.82 us: body(): lax.ppermute(half(part, 1 - which), TENSOR, perm)]
    pallas_call x0 -> x2, Pallas kernels: none -> 11.3 us  [perturbed(): pl.pallas_call(perturb_kernel(first, strides, block, 16, (row_names, rows...]
    ppermute x8, starting transfers between devices: 26.4 us -> 36.5 us  [body(): lax.ppermute(one, TENSOR, perm)]
    all_to_all x2 -> x1, waiting for transfers between devices: 11.4 us -> 19.8 us  [body(): out = lax.all_to_all(out, ('y', 'x'), 0, 0, tiled=True)]
    ppermute x2 -> x1, starting transfers between devices: 16 us -> 7.94 us  [body(): lax.ppermute(half(out, 1 - z_hi).astype(bf16), 'zh', [(0, 1), (1, 0)])]
    ppermute x8 -> x4, starting transfers between devices: 24 us -> 16.6 us  [body(): other = lax.ppermute(half(part, 1 - which), TENSOR, perm)]
  transfers between devices with their start and end apart: 21 -> 21, of which waited for: 14 -> 10; matrix products, arithmetic and copies ran while one was open for 9% -> 8% of each run, Pallas kernels for 0% -> 6%
where the time goes in v3:
time: 196 us; the launch traced here: 195 us
  starting transfers between devices  99.4 us (51%)
  waiting for transfers between devices  59.3 us (30%)
  Pallas kernels  11.3 us (6%)
  matrix products  10.2 us (5%)
  other arithmetic  6.9 us (4%)
  local copies, waits for them, and re-layouts  4.8 us (2%)
  between operations  2.6 us (1%)
    ppermute x8, starting transfers between devices, body(): lax.ppermute(one, TENSOR, perm)  36.5 us
    all_to_all x1, waiting for transfers between devices, body(): out = lax.all_to_all(out, ('y', 'x'), 0, 0, tiled=True)  19.8 us
    ppermute x8, waiting for transfers between devices, body(): lax.ppermute(one, TENSOR, perm)  19 us
    ppermute x4, starting transfers between devices, body(): other = lax.ppermute(half(part, 1 - which), TENSOR, perm)  16.6 us
    all_to_all x1, starting transfers between devices, body(): stats = lax.all_to_all(stats, TENSOR, 0, 0, tiled=True)  14 us
    pallas_call x2, Pallas kernels, perturbed(): pl.pallas_call(perturb_kernel(first, strides, block, 16, (row_names, rows...  11.3 us
    ppermute x4, starting transfers between devices, body(): lax.ppermute(half(part, 1 - which), TENSOR, perm)  11.1 us
    ppermute x4, waiting for transfers between devices, body(): lax.ppermute(half(part, 1 - which), TENSOR, perm)  9.82 us
  transfers between devices with their start and end apart: 21, of which 10 were waited for; matrix products, arithmetic and copies ran while one was open for 8% of the time, Pallas kernels for 6%

profile of v3, /device:TPU:1, one launch (start us, length us, event | category | flops | bytes accessed | tf_op | source)
XLA Modules:
  0.0 194.6 jit_solution(15023474437536548518)
XLA Ops:
  3.8 14.0 %all-to-all-start = ((f32[16,2,512]{2,1,0:T(2,128)}), f32[16,2,512]{2,1,0:T(2,128)S(1)}, u32[]{:S(2)}, u32[]{:S(2)}) async-start(f32[16,2,512]{2,1,0:T(2,128)} %broadcast_in_dim.42), calls=%async_computation | async-start | bytes 131072 | tf_op jit(solution)/shard_map/all_to_all | solution.py:141
  19.1 5.7 %shard_map.122 = (bf16[576,1152]{1,0:T(8,128)(2,1)}, bf16[576,1152]{1,0:T(8,128)(2,1)}) custom-call(s32[2]{0:T(128)} %seeds.3, s32[3]{0:T(128)} %mults.3, f32[1]{0:T(128)S(6)} %copy.33.step, f32[1]{0:T(128)S(6)} %copy.34.scale, bf16[576,1152]{1,0:T(8,128)(2,1)} %weight.1), custom_call_target="tpu_custom_call" | custom-call | tf_op jit(solution)/shard_map/pallas_call | solution.py:77
  26.9 2.0 %collective-permute-start.2 = (f32[8,2304]{1,0:T(8,128)S(1)}, f32[8,2304]{1,0:T(8,128)S(1)}, u32[]{:S(2)}, u32[]{:S(2)}) collective-permute-start(f32[8,2304]{1,0:T(8,128)S(1)} %pad_maximum_fusion.1), channel_id=1, source_target_pairs={{0,1},{1,0},{2,3},{3,2},{4,5},{5,4},{6,7},{7,6},{8,9},{9,8},{10,11... | collective-permute-start | bytes 221192 | tf_op jit(solution)/shard_map/ppermute | solution.py:160
  29.0 2.3 %convolution_convert_fusion.1 = bf16[512,1152]{1,0:T(8,128)(2,1)} fusion(bf16[576,1152]{1,0:T(8,128)(2,1)S(1)} %copy-done.2, bf16[512,576]{0,1:T(8,128)(2,1)S(1)} %copy-done, f32[576]{0:T(1024)S(1)} %convert_element_type.133, f32[512]{0:T(512)S(1)} %broadcast_multiply_fusion), kind=kOutput, calls=%fused_computation.1 | convolution fusion | flops 681246720 | bytes 3100928 | tf_op jit(solution)/shard_map/dot_general | solution.py:153
  31.3 1.9 constant_dynamic-slice_fusion.8
  33.2 2.3 %collective-permute-start = (bf16[256,1152]{1,0:T(8,128)(2,1)}, bf16[256,1152]{1,0:T(8,128)(2,1)}, u32[]{:S(2)}, u32[]{:S(2)}) collective-permute-start(bf16[256,1152]{1,0:T(8,128)(2,1)} %constant_dynamic-slice_fusion.8), channel_id=1, source_target_pairs={{0,1},{1,0},{2,3},{3,2},{4,5},{5,4},{6,7},{7,6},{8,9},{9,8},{10,11... | collective-permute-start | bytes 1769480 | tf_op jit(solution)/shard_map/ppermute | solution.py:159
  36.9 2.2 %collective-permute-start.10 = (bf16[256,1152]{1,0:T(8,128)(2,1)S(1)}, bf16[256,1152]{1,0:T(8,128)(2,1)}, u32[]{:S(2)}, u32[]{:S(2)}) collective-permute-start(bf16[256,1152]{1,0:T(8,128)(2,1)S(1)} %constant_dynamic-slice_fusion.4), channel_id=1, source_target_pairs={{0,1},{1,0},{2,3},{3,2},{4,5},{5,4},{6,7},{7,6},{8,9},{9,8},{10,11... | collective-permute-start | bytes 1769480 | tf_op jit(solution)/shard_map/ppermute | solution.py:159
  39.2 4.4 %collective-permute-start.3 = (f32[8,2304]{1,0:T(8,128)S(1)}, f32[8,2304]{1,0:T(8,128)S(1)}, u32[]{:S(2)}, u32[]{:S(2)}) collective-permute-start(f32[8,2304]{1,0:T(8,128)S(1)} %fusion.58), channel_id=1, source_target_pairs={{0,2},{1,5},{2,0},{3,7},{4,6},{5,1},{6,4},{7,3},{8,10},{9,13},{10,... | collective-permute-start | bytes 221192 | tf_op jit(solution)/shard_map/ppermute | solution.py:183
  48.2 4.8 %collective-permute-start.1 = (bf16[128,1152]{1,0:T(8,128)(2,1)S(1)}, bf16[128,1152]{1,0:T(8,128)(2,1)S(1)}, u32[]{:S(2)}, u32[]{:S(2)}) collective-permute-start(bf16[128,1152]{1,0:T(8,128)(2,1)S(1)} %constant_dynamic-slice_fusion.7), channel_id=1, source_target_pairs={{0,2},{1,5},{2,0},{3,7},{4,6},{5,1},{6,4},{7,3},{8,10},{9,13},{10,... | collective-permute-start | bytes 884744 | tf_op jit(solution)/shard_map/ppermute | solution.py:182
  54.2 1.9 collective-permute-start.11
  56.1 3.6 %collective-permute-done.1 = bf16[128,1152]{1,0:T(8,128)(2,1)S(1)} collective-permute-done((bf16[128,1152]{1,0:T(8,128)(2,1)S(1)}, bf16[128,1152]{1,0:T(8,128)(2,1)S(1)}, u32[]{:S(2)}, u32[]{:S(2)}) %collective-permute-start.1) | collective-permute-done | bytes 294944 | tf_op jit(solution)/shard_map/ppermute | solution.py:182
  59.7 6.2 %collective-permute-done.11 = bf16[128,1152]{1,0:T(8,128)(2,1)S(1)} collective-permute-done((bf16[128,1152]{1,0:T(8,128)(2,1)S(1)}, bf16[128,1152]{1,0:T(8,128)(2,1)S(1)}, u32[]{:S(2)}, u32[]{:S(2)}) %collective-permute-start.11) | collective-permute-done | bytes 294944 | tf_op jit(solution)/shard_map/ppermute | solution.py:182
  66.3 3.4 %collective-permute-start.4 = (bf16[64,1152]{1,0:T(8,128)(2,1)S(1)}, bf16[64,1152]{1,0:T(8,128)(2,1)S(1)}, u32[]{:S(2)}, u32[]{:S(2)}) collective-permute-start(bf16[64,1152]{1,0:T(8,128)(2,1)S(1)} %constant_dynamic-slice_fusion.6), channel_id=1, source_target_pairs={{0,4},{1,3},{2,6},{3,1},{4,0},{5,7},{6,2},{7,5},{8,12},{9,11},{10,... | collective-permute-start | bytes 442376 | tf_op jit(solution)/shard_map/ppermute | solution.py:197
  69.7 1.9 collective-permute-start.12
  72.2 7.0 %collective-permute-start.5 = (bf16[32,1152]{1,0:T(8,128)(2,1)S(1)}, bf16[32,1152]{1,0:T(8,128)(2,1)S(1)}, u32[]{:S(2)}, u32[]{:S(2)}) collective-permute-start(bf16[32,1152]{1,0:T(8,128)(2,1)S(1)} %constant_dynamic-slice_fusion.5), channel_id=1, source_target_pairs={{0,8},{1,9},{2,10},{3,11},{4,12},{5,13},{6,14},{7,15},{8,0},{9,1},... | collective-permute-start | bytes 221192 | tf_op jit(solution)/shard_map/ppermute | solution.py:197
  79.3 4.3 %collective-permute-start.13 = (bf16[32,1152]{1,0:T(8,128)(2,1)S(1)}, bf16[32,1152]{1,0:T(8,128)(2,1)S(1)}, u32[]{:S(2)}, u32[]{:S(2)}) collective-permute-start(bf16[32,1152]{1,0:T(8,128)(2,1)S(1)} %constant_dynamic-slice_fusion.1), channel_id=1, source_target_pairs={{0,8},{1,9},{2,10},{3,11},{4,12},{5,13},{6,14},{7,15},{8,0},{9,1},... | collective-permute-start | bytes 221192 | tf_op jit(solution)/shard_map/ppermute | solution.py:197
  83.7 4.9 %collective-permute-start.6 = (bf16[32,1152]{1,0:T(8,128)(2,1)S(1)}, bf16[32,1152]{1,0:T(8,128)(2,1)S(1)}, u32[]{:S(2)}, u32[]{:S(2)}) collective-permute-start(bf16[32,1152]{1,0:T(8,128)(2,1)S(1)} %maximum_convert_fusion.1), channel_id=1, source_target_pairs={{0,8},{1,9},{2,10},{3,11},{4,12},{5,13},{6,14},{7,15},{8,0},{9,1},... | collective-permute-start | bytes 221192 | tf_op jit(solution)/shard_map/ppermute | solution.py:203
  88.6 2.7 %collective-permute-done.13 = bf16[32,1152]{1,0:T(8,128)(2,1)S(1)} collective-permute-done((bf16[32,1152]{1,0:T(8,128)(2,1)S(1)}, bf16[32,1152]{1,0:T(8,128)(2,1)S(1)}, u32[]{:S(2)}, u32[]{:S(2)}) %collective-permute-start.13) | collective-permute-done | bytes 73760 | tf_op jit(solution)/shard_map/ppermute | solution.py:197
  93.2 9.1 %collective-permute-done.6 = bf16[32,1152]{1,0:T(8,128)(2,1)S(1)} collective-permute-done((bf16[32,1152]{1,0:T(8,128)(2,1)S(1)}, bf16[32,1152]{1,0:T(8,128)(2,1)S(1)}, u32[]{:S(2)}, u32[]{:S(2)}) %collective-permute-start.6) | collective-permute-done | bytes 73760 | tf_op jit(solution)/shard_map/ppermute | solution.py:203
  102.4 1.9 collective-permute-start.7
  104.3 3.4 %collective-permute-start.15 = (bf16[64,1152]{1,0:T(8,128)(2,1)S(1)}, bf16[64,1152]{1,0:T(8,128)(2,1)S(1)}, u32[]{:S(2)}, u32[]{:S(2)}) collective-permute-start(bf16[64,1152]{1,0:T(8,128)(2,1)S(1)} %maximum_select_fusion.9), channel_id=1, source_target_pairs={{0,4},{1,3},{2,6},{3,1},{4,0},{5,7},{6,2},{7,5},{8,12},{9,11},{10,... | collective-permute-start | bytes 442376 | tf_op jit(solution)/shard_map/ppermute | solution.py:203
  108.3 8.6 %collective-permute-start.8 = (bf16[128,1152]{1,0:T(8,128)(2,1)S(1)}, bf16[128,1152]{1,0:T(8,128)(2,1)S(1)}, u32[]{:S(2)}, u32[]{:S(2)}) collective-permute-start(bf16[128,1152]{1,0:T(8,128)(2,1)S(1)} %maximum_select_fusion.6), channel_id=1, source_target_pairs={{0,2},{1,5},{2,0},{3,7},{4,6},{5,1},{6,4},{7,3},{8,10},{9,13},{10,... | collective-permute-start | bytes 884744 | tf_op jit(solution)/shard_map/ppermute | solution.py:203
  117.0 5.1 %collective-permute-start.16 = (bf16[128,1152]{1,0:T(8,128)(2,1)S(1)}, bf16[128,1152]{1,0:T(8,128)(2,1)S(1)}, u32[]{:S(2)}, u32[]{:S(2)}) collective-permute-start(bf16[128,1152]{1,0:T(8,128)(2,1)S(1)} %maximum_select_fusion.7), channel_id=1, source_target_pairs={{0,2},{1,5},{2,0},{3,7},{4,6},{5,1},{6,4},{7,3},{8,10},{9,13},{10,... | collective-permute-start | bytes 884744 | tf_op jit(solution)/shard_map/ppermute | solution.py:203
  122.1 9.4 %collective-permute-done.8 = bf16[128,1152]{1,0:T(8,128)(2,1)S(1)} collective-permute-done((bf16[128,1152]{1,0:T(8,128)(2,1)S(1)}, bf16[128,1152]{1,0:T(8,128)(2,1)S(1)}, u32[]{:S(2)}, u32[]{:S(2)}) %collective-permute-start.8) | collective-permute-done | bytes 294944 | tf_op jit(solution)/shard_map/ppermute | solution.py:203
  131.6 7.7 %collective-permute-start.9 = (bf16[256,1152]{1,0:T(8,128)(2,1)S(1)}, bf16[256,1152]{1,0:T(8,128)(2,1)S(1)}, u32[]{:S(2)}, u32[]{:S(2)}) collective-permute-start(bf16[256,1152]{1,0:T(8,128)(2,1)S(1)} %maximum_select_fusion.4), channel_id=1, source_target_pairs={{0,1},{1,0},{2,3},{3,2},{4,5},{5,4},{6,7},{7,6},{8,9},{9,8},{10,11... | collective-permute-start | bytes 1769480 | tf_op jit(solution)/shard_map/ppermute | solution.py:203
  139.5 3.0 %collective-permute-start.17 = (bf16[256,1152]{1,0:T(8,128)(2,1)S(1)}, bf16[256,1152]{1,0:T(8,128)(2,1)S(1)}, u32[]{:S(2)}, u32[]{:S(2)}) collective-permute-start(bf16[256,1152]{1,0:T(8,128)(2,1)S(1)} %maximum_select_fusion.5), channel_id=1, source_target_pairs={{0,1},{1,0},{2,3},{3,2},{4,5},{5,4},{6,7},{7,6},{8,9},{9,8},{10,11... | collective-permute-start | bytes 1769480 | tf_op jit(solution)/shard_map/ppermute | solution.py:203
  142.5 5.7 %shard_map.123 = (bf16[576,1152]{1,0:T(8,128)(2,1)}, bf16[576,1152]{1,0:T(8,128)(2,1)}) custom-call(s32[2]{0:T(128)} %seeds.3, s32[3]{0:T(128)} %mults.3, f32[1]{0:T(128)S(6)} %copy.33.step, f32[1]{0:T(128)S(6)} %copy.34.scale, bf16[576,1152]{1,0:T(8,128)(2,1)} %bitcast.22), custom_call_target="tpu_custom_call" | custom-call | tf_op jit(solution)/shard_map/pallas_call | solution.py:77
  148.2 2.4 %convolution_convert_fusion.3 = bf16[512,576]{0,1:T(8,128)(2,1)S(1)} fusion(bf16[576,1152]{1,0:T(8,128)(2,1)} %get-tuple-element.9, bf16[256,1152]{1,0:T(8,128)(2,1)S(1)} %collective-permute-done.9, bf16[256,1152]{1,0:T(8,128)(2,1)S(1)} %maximum_select_fusion.4, pred[]{:T(512)S(6)} %eq.50), kind=kOutput, calls=%fused_computation.8 | convolution fusion | flops 685080576 | bytes 3096577 | tf_op jit(solution)/shard_map/dot_general | solution.py:206
  153.5 6.8 %all-to-all-start.1 = ((bf16[16,32,1152]{2,1,0:T(8,128)(2,1)}), bf16[16,32,1152]{2,1,0:T(8,128)(2,1)S(1)}, u32[]{:S(2)}, u32[]{:S(2)}) async-start(bf16[16,32,1152]{2,1,0:T(8,128)(2,1)} %bitcast.8), calls=%async_computation.1 | async-start | bytes 2359296 | tf_op jit(solution)/shard_map/all_to_all | solution.py:213
  160.3 19.8 %all-to-all-done.1 = bf16[16,32,1152]{2,1,0:T(8,128)(2,1)S(1)} async-done(((bf16[16,32,1152]{2,1,0:T(8,128)(2,1)}), bf16[16,32,1152]{2,1,0:T(8,128)(2,1)S(1)}, u32[]{:S(2)}, u32[]{:S(2)}) %all-to-all-start.1) | async-done | bytes 1179680 | tf_op jit(solution)/shard_map/all_to_all | solution.py:213
  180.4 7.9 %collective-permute-start.18 = (bf16[16,1152]{1,0:T(8,128)(2,1)S(1)}, bf16[16,1152]{1,0:T(8,128)(2,1)S(1)}, u32[]{:S(2)}, u32[]{:S(2)}) collective-permute-start(bf16[16,1152]{1,0:T(8,128)(2,1)S(1)} %dynamic-slice_convert_fusion), channel_id=1, source_target_pairs={{0,64},{64,0},{1,65},{65,1},{2,66},{66,2},{3,67},{67,3},{4,68},{68... | collective-permute-start | bytes 110600 | tf_op jit(solution)/shard_map/ppermute | solution.py:215
  188.3 5.5 %collective-permute-done.18 = bf16[16,1152]{1,0:T(8,128)(2,1)S(1)} collective-permute-done((bf16[16,1152]{1,0:T(8,128)(2,1)S(1)}, bf16[16,1152]{1,0:T(8,128)(2,1)S(1)}, u32[]{:S(2)}, u32[]{:S(2)}) %collective-permute-start.18) | collective-permute-done | bytes 36896 | tf_op jit(solution)/shard_map/ppermute | solution.py:215
  (87 shorter events, 20.1 us)
Async XLA Ops:
  1.8 22.9 %copy-start.4 = (bf16[576]{0:T(1024)(128)(2,1)S(1)}, bf16[576]{0:T(1024)(128)(2,1)}, u32[]{:S(2)}) copy-start(bf16[576]{0:T(1024)(128)(2,1)} %param.12) | copy-start | bytes 3460
  1.8 22.9 %copy-start.5 = (bf16[576]{0:T(1024)(128)(2,1)S(1)}, bf16[576]{0:T(1024)(128)(2,1)}, u32[]{:S(2)}) copy-start(bf16[576]{0:T(1024)(128)(2,1)} %param.13) | copy-start | bytes 3460
  3.8 41.7 %all-to-all-start = ((f32[16,2,512]{2,1,0:T(2,128)}), f32[16,2,512]{2,1,0:T(2,128)S(1)}, u32[]{:S(2)}, u32[]{:S(2)}) async-start(f32[16,2,512]{2,1,0:T(2,128)} %broadcast_in_dim.42), calls=%async_computation | async-start | bytes 131072 | tf_op jit(solution)/shard_map/all_to_all | solution.py:141
  24.8 1.8 copy-start.2
  24.8 4.2 %copy-start = (bf16[512,576]{0,1:T(8,128)(2,1)S(1)}, bf16[512,576]{0,1:T(8,128)(2,1)}, u32[]{:S(2)}) copy-start(bf16[512,576]{0,1:T(8,128)(2,1)} %param.11) | copy-start | bytes 1769476
  26.9 12.2 %collective-permute-start.2 = (f32[8,2304]{1,0:T(8,128)S(1)}, f32[8,2304]{1,0:T(8,128)S(1)}, u32[]{:S(2)}, u32[]{:S(2)}) collective-permute-start(f32[8,2304]{1,0:T(8,128)S(1)} %pad_maximum_fusion.1), channel_id=1, source_target_pairs={{0,1},{1,0},{2,3},{3,2},{4,5},{5,4},{6,7},{7,6},{8,9},{9,8},{10,11... | collective-permute-start | bytes 221192 | tf_op jit(solution)/shard_map/ppermute | solution.py:160
  29.0 6.6 %copy-start.1 = (bf16[576,1152]{1,0:T(8,128)(2,1)S(1)}, bf16[576,1152]{1,0:T(8,128)(2,1)}, u32[]{:S(2)}) copy-start(bf16[576,1152]{1,0:T(8,128)(2,1)} %get-tuple-element.8) | copy-start | bytes 3981316
  33.2 13.7 %collective-permute-start = (bf16[256,1152]{1,0:T(8,128)(2,1)}, bf16[256,1152]{1,0:T(8,128)(2,1)}, u32[]{:S(2)}, u32[]{:S(2)}) collective-permute-start(bf16[256,1152]{1,0:T(8,128)(2,1)} %constant_dynamic-slice_fusion.8), channel_id=1, source_target_pairs={{0,1},{1,0},{2,3},{3,2},{4,5},{5,4},{6,7},{7,6},{8,9},{9,8},{10,11... | collective-permute-start | bytes 1769480 | tf_op jit(solution)/shard_map/ppermute | solution.py:159
  36.8 2.3 %copy-start.6 = (bf16[1152]{0:T(1024)(128)(2,1)S(1)}, bf16[1152]{0:T(1024)(128)(2,1)}, u32[]{:S(2)}) copy-start(bf16[1152]{0:T(1024)(128)(2,1)} %param.15) | copy-start | bytes 6916
  36.9 10.0 %copy-start.3 = (bf16[512,1152]{1,0:T(8,128)(2,1)S(1)}, bf16[512,1152]{1,0:T(8,128)(2,1)}, u32[]{:S(2)}) copy-start(bf16[512,1152]{1,0:T(8,128)(2,1)} %convolution_convert_fusion.1) | copy-start | bytes 3538948
  36.9 16.0 %collective-permute-start.10 = (bf16[256,1152]{1,0:T(8,128)(2,1)S(1)}, bf16[256,1152]{1,0:T(8,128)(2,1)}, u32[]{:S(2)}, u32[]{:S(2)}) collective-permute-start(bf16[256,1152]{1,0:T(8,128)(2,1)S(1)} %constant_dynamic-slice_fusion.4), channel_id=1, source_target_pairs={{0,1},{1,0},{2,3},{3,2},{4,5},{5,4},{6,7},{7,6},{8,9},{9,8},{10,11... | collective-permute-start | bytes 1769480 | tf_op jit(solution)/shard_map/ppermute | solution.py:159
  39.2 6.3 %collective-permute-start.3 = (f32[8,2304]{1,0:T(8,128)S(1)}, f32[8,2304]{1,0:T(8,128)S(1)}, u32[]{:S(2)}, u32[]{:S(2)}) collective-permute-start(f32[8,2304]{1,0:T(8,128)S(1)} %fusion.58), channel_id=1, source_target_pairs={{0,2},{1,5},{2,0},{3,7},{4,6},{5,1},{6,4},{7,3},{8,10},{9,13},{10,... | collective-permute-start | bytes 221192 | tf_op jit(solution)/shard_map/ppermute | solution.py:183
  48.2 11.6 %collective-permute-start.1 = (bf16[128,1152]{1,0:T(8,128)(2,1)S(1)}, bf16[128,1152]{1,0:T(8,128)(2,1)S(1)}, u32[]{:S(2)}, u32[]{:S(2)}) collective-permute-start(bf16[128,1152]{1,0:T(8,128)(2,1)S(1)} %constant_dynamic-slice_fusion.7), channel_id=1, source_target_pairs={{0,2},{1,5},{2,0},{3,7},{4,6},{5,1},{6,4},{7,3},{8,10},{9,13},{10,... | collective-permute-start | bytes 884744 | tf_op jit(solution)/shard_map/ppermute | solution.py:182
  54.2 11.8 %collective-permute-start.11 = (bf16[128,1152]{1,0:T(8,128)(2,1)S(1)}, bf16[128,1152]{1,0:T(8,128)(2,1)S(1)}, u32[]{:S(2)}, u32[]{:S(2)}) collective-permute-start(bf16[128,1152]{1,0:T(8,128)(2,1)S(1)} %constant_dynamic-slice_fusion.3), channel_id=1, source_target_pairs={{0,2},{1,5},{2,0},{3,7},{4,6},{5,1},{6,4},{7,3},{8,10},{9,13},{10,... | collective-permute-start | bytes 884744 | tf_op jit(solution)/shard_map/ppermute | solution.py:182
  66.3 5.9 %collective-permute-start.4 = (bf16[64,1152]{1,0:T(8,128)(2,1)S(1)}, bf16[64,1152]{1,0:T(8,128)(2,1)S(1)}, u32[]{:S(2)}, u32[]{:S(2)}) collective-permute-start(bf16[64,1152]{1,0:T(8,128)(2,1)S(1)} %constant_dynamic-slice_fusion.6), channel_id=1, source_target_pairs={{0,4},{1,3},{2,6},{3,1},{4,0},{5,7},{6,2},{7,5},{8,12},{9,11},{10,... | collective-permute-start | bytes 442376 | tf_op jit(solution)/shard_map/ppermute | solution.py:197
  69.7 9.6 %collective-permute-start.12 = (bf16[64,1152]{1,0:T(8,128)(2,1)S(1)}, bf16[64,1152]{1,0:T(8,128)(2,1)S(1)}, u32[]{:S(2)}, u32[]{:S(2)}) collective-permute-start(bf16[64,1152]{1,0:T(8,128)(2,1)S(1)} %constant_dynamic-slice_fusion.2), channel_id=1, source_target_pairs={{0,4},{1,3},{2,6},{3,1},{4,0},{5,7},{6,2},{7,5},{8,12},{9,11},{10,... | collective-permute-start | bytes 442376 | tf_op jit(solution)/shard_map/ppermute | solution.py:197
  72.2 11.4 %collective-permute-start.5 = (bf16[32,1152]{1,0:T(8,128)(2,1)S(1)}, bf16[32,1152]{1,0:T(8,128)(2,1)S(1)}, u32[]{:S(2)}, u32[]{:S(2)}) collective-permute-start(bf16[32,1152]{1,0:T(8,128)(2,1)S(1)} %constant_dynamic-slice_fusion.5), channel_id=1, source_target_pairs={{0,8},{1,9},{2,10},{3,11},{4,12},{5,13},{6,14},{7,15},{8,0},{9,1},... | collective-permute-start | bytes 221192 | tf_op jit(solution)/shard_map/ppermute | solution.py:197
  79.3 11.9 %collective-permute-start.13 = (bf16[32,1152]{1,0:T(8,128)(2,1)S(1)}, bf16[32,1152]{1,0:T(8,128)(2,1)S(1)}, u32[]{:S(2)}, u32[]{:S(2)}) collective-permute-start(bf16[32,1152]{1,0:T(8,128)(2,1)S(1)} %constant_dynamic-slice_fusion.1), channel_id=1, source_target_pairs={{0,8},{1,9},{2,10},{3,11},{4,12},{5,13},{6,14},{7,15},{8,0},{9,1},... | collective-permute-start | bytes 221192 | tf_op jit(solution)/shard_map/ppermute | solution.py:197
  83.7 18.6 %collective-permute-start.6 = (bf16[32,1152]{1,0:T(8,128)(2,1)S(1)}, bf16[32,1152]{1,0:T(8,128)(2,1)S(1)}, u32[]{:S(2)}, u32[]{:S(2)}) collective-permute-start(bf16[32,1152]{1,0:T(8,128)(2,1)S(1)} %maximum_convert_fusion.1), channel_id=1, source_target_pairs={{0,8},{1,9},{2,10},{3,11},{4,12},{5,13},{6,14},{7,15},{8,0},{9,1},... | collective-permute-start | bytes 221192 | tf_op jit(solution)/shard_map/ppermute | solution.py:203
  91.3 13.0 %collective-permute-start.14 = (bf16[32,1152]{1,0:T(8,128)(2,1)S(1)}, bf16[32,1152]{1,0:T(8,128)(2,1)S(1)}, u32[]{:S(2)}, u32[]{:S(2)}) collective-permute-start(bf16[32,1152]{1,0:T(8,128)(2,1)S(1)} %maximum_convert_fusion), channel_id=1, source_target_pairs={{0,8},{1,9},{2,10},{3,11},{4,12},{5,13},{6,14},{7,15},{8,0},{9,1},... | collective-permute-start | bytes 221192 | tf_op jit(solution)/shard_map/ppermute | solution.py:203
  102.4 5.9 %collective-permute-start.7 = (bf16[64,1152]{1,0:T(8,128)(2,1)S(1)}, bf16[64,1152]{1,0:T(8,128)(2,1)S(1)}, u32[]{:S(2)}, u32[]{:S(2)}) collective-permute-start(bf16[64,1152]{1,0:T(8,128)(2,1)S(1)} %maximum_select_fusion.8), channel_id=1, source_target_pairs={{0,4},{1,3},{2,6},{3,1},{4,0},{5,7},{6,2},{7,5},{8,12},{9,11},{10,... | collective-permute-start | bytes 442376 | tf_op jit(solution)/shard_map/ppermute | solution.py:203
  104.3 12.6 %collective-permute-start.15 = (bf16[64,1152]{1,0:T(8,128)(2,1)S(1)}, bf16[64,1152]{1,0:T(8,128)(2,1)S(1)}, u32[]{:S(2)}, u32[]{:S(2)}) collective-permute-start(bf16[64,1152]{1,0:T(8,128)(2,1)S(1)} %maximum_select_fusion.9), channel_id=1, source_target_pairs={{0,4},{1,3},{2,6},{3,1},{4,0},{5,7},{6,2},{7,5},{8,12},{9,11},{10,... | collective-permute-start | bytes 442376 | tf_op jit(solution)/shard_map/ppermute | solution.py:203
  108.3 23.2 %collective-permute-start.8 = (bf16[128,1152]{1,0:T(8,128)(2,1)S(1)}, bf16[128,1152]{1,0:T(8,128)(2,1)S(1)}, u32[]{:S(2)}, u32[]{:S(2)}) collective-permute-start(bf16[128,1152]{1,0:T(8,128)(2,1)S(1)} %maximum_select_fusion.6), channel_id=1, source_target_pairs={{0,2},{1,5},{2,0},{3,7},{4,6},{5,1},{6,4},{7,3},{8,10},{9,13},{10,... | collective-permute-start | bytes 884744 | tf_op jit(solution)/shard_map/ppermute | solution.py:203
  117.0 22.3 %collective-permute-start.16 = (bf16[128,1152]{1,0:T(8,128)(2,1)S(1)}, bf16[128,1152]{1,0:T(8,128)(2,1)S(1)}, u32[]{:S(2)}, u32[]{:S(2)}) collective-permute-start(bf16[128,1152]{1,0:T(8,128)(2,1)S(1)} %maximum_select_fusion.7), channel_id=1, source_target_pairs={{0,2},{1,5},{2,0},{3,7},{4,6},{5,1},{6,4},{7,3},{8,10},{9,13},{10,... | collective-permute-start | bytes 884744 | tf_op jit(solution)/shard_map/ppermute | solution.py:203
  131.6 16.6 %collective-permute-start.9 = (bf16[256,1152]{1,0:T(8,128)(2,1)S(1)}, bf16[256,1152]{1,0:T(8,128)(2,1)S(1)}, u32[]{:S(2)}, u32[]{:S(2)}) collective-permute-start(bf16[256,1152]{1,0:T(8,128)(2,1)S(1)} %maximum_select_fusion.4), channel_id=1, source_target_pairs={{0,1},{1,0},{2,3},{3,2},{4,5},{5,4},{6,7},{7,6},{8,9},{9,8},{10,11... | collective-permute-start | bytes 1769480 | tf_op jit(solution)/shard_map/ppermute | solution.py:203
  139.5 11.1 %collective-permute-start.17 = (bf16[256,1152]{1,0:T(8,128)(2,1)S(1)}, bf16[256,1152]{1,0:T(8,128)(2,1)S(1)}, u32[]{:S(2)}, u32[]{:S(2)}) collective-permute-start(bf16[256,1152]{1,0:T(8,128)(2,1)S(1)} %maximum_select_fusion.5), channel_id=1, source_target_pairs={{0,1},{1,0},{2,3},{3,2},{4,5},{5,4},{6,7},{7,6},{8,9},{9,8},{10,11... | collective-permute-start | bytes 1769480 | tf_op jit(solution)/shard_map/ppermute | solution.py:203
  148.2 2.4 %copy-start.8 = (bf16[576,1152]{1,0:T(8,128)(2,1)S(1)}, bf16[576,1152]{1,0:T(8,128)(2,1)}, u32[]{:S(2)}) copy-start(bf16[576,1152]{1,0:T(8,128)(2,1)} %get-tuple-element.11) | copy-start | bytes 3981316
  153.5 26.6 %all-to-all-start.1 = ((bf16[16,32,1152]{2,1,0:T(8,128)(2,1)}), bf16[16,32,1152]{2,1,0:T(8,128)(2,1)S(1)}, u32[]{:S(2)}, u32[]{:S(2)}) async-start(bf16[16,32,1152]{2,1,0:T(8,128)(2,1)} %bitcast.8), calls=%async_computation.1 | async-start | bytes 2359296 | tf_op jit(solution)/shard_map/all_to_all | solution.py:213
  160.3 28.0 %copy-start.7 = (bf16[576]{0:T(1024)(128)(2,1)S(1)}, bf16[576]{0:T(1024)(128)(2,1)}, u32[]{:S(2)}) copy-start(bf16[576]{0:T(1024)(128)(2,1)} %param.17) | copy-start | bytes 3460
  180.4 13.5 %collective-permute-start.18 = (bf16[16,1152]{1,0:T(8,128)(2,1)S(1)}, bf16[16,1152]{1,0:T(8,128)(2,1)S(1)}, u32[]{:S(2)}, u32[]{:S(2)}) collective-permute-start(bf16[16,1152]{1,0:T(8,128)(2,1)S(1)} %dynamic-slice_convert_fusion), channel_id=1, source_target_pairs={{0,64},{64,0},{1,65},{65,1},{2,66},{66,2},{3,67},{67,3},{4,68},{68... | collective-permute-start | bytes 110600 | tf_op jit(solution)/shard_map/ppermute | solution.py:215

commit v4 on v3

--- a/solution.py
+++ b/solution.py
@@ -90,6 +90,8 @@
 
 
 STAGES = [(0, 1), (1, 0), (2, 2)]
+STEPS = 7
+TIES = {1: 2, 2: 3, 3: 4}
 CORE_SWAP = [(i, i ^ 1) for i in range(16)]
 
 
@@ -139,84 +141,67 @@
     local_sq = jnp.sum(offset * offset, axis=1)
     stats = jnp.broadcast_to(jnp.stack([local_mean, local_sq])[None], (16, 2, tokens.shape[0]))
     stats = lax.all_to_all(stats, TENSOR, 0, 0, tiled=True)
-    scaled = (offset * ln_gain.astype(f32)).astype(bf16)
-    slot = lax.broadcasted_iota(jnp.int32, (8, feat_local), 0)
-    pair = jnp.where(slot == core, ln_gain[None], 0) + jnp.where(slot == 2, ln_bias[None], 0)
-    pair = pair.astype(bf16)
-
-    scalars = (step_seeds, hash_mults, update_step, perturb_scale)
-    first_weights = perturbed(fc1_weight, 0, (FF, 1), TENSOR, FSDP, scalars, 4)
-    second_weights = perturbed(fc2_weight.T, D * FF, (1, D), TENSOR, FSDP, scalars, 4)
-    bias_one = fc1_bias.astype(f32)
-    bias_two = fc2_bias.astype(f32)
-
-    parts = [jnp.dot(scaled, w, preferred_element_type=f32).astype(bf16) for w in first_weights]
-    sides = jnp.concatenate(
-        [jnp.dot(pair, w, preferred_element_type=f32) for w in first_weights], axis=1
-    )
-
-    which, perm = picks[0]
-    others = [lax.ppermute(half(part, 1 - which), TENSOR, perm) for part in parts]
-    sides = sides + lax.ppermute(sides, TENSOR, perm)
-    parts = [
-        (half(part, which).astype(f32) + other.astype(f32)).astype(bf16)
-        for part, other in zip(parts, others)
-    ]
-
-    which, perm = picks[1]
-    rows = tokens.shape[0] // 4
-    stats = lax.dynamic_slice_in_dim(stats, core * 2 * rows + which * rows, rows, 2)
     means = stats[:, 0]
     row_mean = jnp.mean(means, axis=0)
     spread = means - row_mean[None]
-    row_var = jnp.sum(stats[:, 1] + feat_local * spread * spread, axis=0) / D
-    row_scale = lax.rsqrt(row_var + 1e-05)[:, None]
-    far = z_lo ^ jnp.where(core == 0, 1 << STAGES[0][0], 1 << STAGES[0][1])
-    chips = lax.broadcasted_iota(jnp.int32, (16, rows), 0)
-    near_rows = jnp.where(lax.shift_right_logical(chips, 1) == z_lo, spread, 0)
-    far_rows = jnp.where(lax.shift_right_logical(chips, 1) == far, spread, 0)
-    fold = lambda one: jnp.sum(one.reshape(8, 2, rows), axis=0)
-    gap = jnp.zeros((6, rows), f32)
-    spread = jnp.concatenate([fold(near_rows), gap, fold(far_rows), gap], axis=0)
-
-    others = [lax.ppermute(half(part, 1 - which), TENSOR, perm) for part in parts]
-    far_sides = lax.ppermute(sides, TENSOR, perm)
-    both = jnp.concatenate([sides, far_sides], axis=0)
-    shift = lax.dot_general(
-        spread, both, (((0,), (0,)), ((), ())), precision=lax.Precision.HIGHEST
-    )
-    bias_sum = both[2:3] + both[10:11]
-    for sign in range(2):
-        columns = slice(sign * unit_local, (sign + 1) * unit_local)
-        part = half(parts[sign], which).astype(f32) + others[sign].astype(f32)
-        parts[sign] = (row_scale * (part + shift[:, columns]) + bias_sum[:, columns]).astype(bf16)
-
-    hidden = []
-    for part in parts:
-        for which, perm in picks[2:]:
-            other = lax.ppermute(half(part, 1 - which), TENSOR, perm)
+    row_var = (jnp.sum(stats[:, 1] + feat_local * spread * spread, axis=0) / D)[:, None]
+    centered = values - row_mean[:, None]
+    normed = (
+        centered * lax.rsqrt(row_var + 1e-05) * ln_gain.astype(f32) + ln_bias.astype(f32)
+    ).astype(bf16)
+    normed = lax.optimization_barrier(normed)
+
+    scalars = (step_seeds, hash_mults, update_step, perturb_scale)
+    first_weights = perturbed(fc1_weight, 0, (FF, 1), TENSOR, FSDP, scalars, 4)
+    bias_one = fc1_bias.astype(f32)
+    bias_two = fc2_bias.astype(f32)
+
+    def stream(sign):
+        part = jnp.dot(normed, first_weights[sign], preferred_element_type=f32).astype(bf16)
+        for which, perm in picks[:3]:
+            send = yield half(part, 1 - which)
+            other = lax.ppermute(send, TENSOR, perm)
             part = (half(part, which).astype(f32) + other.astype(f32)).astype(bf16)
-        if hidden:
-            part = after(part, hidden[0])
-        hidden.append(jax.nn.relu(part.astype(f32) + bias_one).astype(bf16))
-    for which, perm in picks[::-1]:
-        hidden = [join(one, lax.ppermute(one, TENSOR, perm), which) for one in hidden]
-    out = jnp.concatenate(
-        [
-            jnp.dot(one, weight.T, preferred_element_type=f32).astype(bf16)
-            for one, weight in zip(hidden, second_weights)
-        ],
-        axis=1,
-    )
-    width = 2 * feat_local
-    out = out.reshape(4, 2, 4, -1, width).transpose(0, 2, 1, 3, 4).reshape(16, -1, width)
-    out = lax.all_to_all(out, ("y", "x"), 0, 0, tiled=True)
-    out = jnp.sum(out.astype(f32), axis=0)
+        part = yield part
+        other = lax.ppermute(part, TENSOR, picks[3][1])
+        part = jax.nn.relu(part.astype(f32) + other.astype(f32) + bias_one).astype(bf16)
+        for which, perm in picks[2::-1]:
+            part = yield part
+            part = join(part, lax.ppermute(part, TENSOR, perm), which)
+        out = jnp.dot(part, second_weights[sign].T, preferred_element_type=f32).astype(bf16)
+        yield out
+
+    def scatter(out):
+        out = lax.all_to_all(out, ("y", "x"), 0, 0, tiled=True)
+        return jnp.sum(out.astype(f32), axis=0)
+
+    plus = stream(0)
+    minus = stream(1)
+    ahead = [next(plus)]
+    behind = next(minus)
+    second_weights = []
+    for step in range(STEPS):
+        if step == 4:
+            held = after(fc2_weight.T, ahead[step])
+            second_weights += perturbed(held, D * FF, (1, D), TENSOR, FSDP, scalars, 4)
+        if step == 6:
+            ahead[step] = after(ahead[step], second_weights[0])
+        ahead.append(plus.send(ahead[-1]))
+    for step in range(STEPS):
+        if step in TIES:
+            behind = after(behind, ahead[TIES[step]])
+        behind = minus.send(behind)
+    out = scatter(blocks(jnp.concatenate([ahead[-1], behind], axis=1)))
     other = lax.ppermute(half(out, 1 - z_hi).astype(bf16), "zh", [(0, 1), (1, 0)])
     out = half(out, z_hi) + other.astype(f32)
     branch_plus = (out[:, :feat_local] + bias_two).astype(bf16)
     branch_minus = (out[:, feat_local:] + bias_two).astype(bf16)
     return (branch_plus, branch_minus)
+
+
+def blocks(out):
+    out = out.reshape(4, 2, 4, -1, out.shape[1]).transpose(0, 2, 1, 3, 4)
+    return out.reshape(16, -1, out.shape[-1])
 
 
 def solution(mesh):

time: 196 us -> 166 us (0.85)
  starting transfers between devices: 99.4 us -> 82.7 us
  matrix products: 10.2 us -> 5.65 us
  waiting for transfers between devices: 59.3 us -> 55 us
  local copies, waits for them, and re-layouts: 4.8 us -> 2.75 us
  other arithmetic: 6.9 us -> 4.87 us
    ppermute x18 -> x14, starting transfers between devices: 70.7 us -> 53.9 us  [the longest x6 28.4 us: stream(): part = join(part, lax.ppermute(part, TENSOR, perm), which)]
    ppermute x18 -> x14, waiting for transfers between devices: 33.9 us -> 28.1 us  [the longest x6 21.5 us: stream(): other = lax.ppermute(send, TENSOR, perm)]
    dot_general x7 -> x4, matrix products: 10.2 us -> 5.65 us  [the longest x2 3.71 us: stream(): jnp.dot(normed, first_weights[sign], preferred_element_type=f32)]
    all_to_all x1, waiting for transfers between devices: 0.01 us -> 3.09 us  [body(): stats = lax.all_to_all(stats, TENSOR, 0, 0, tiled=True)]
  transfers between devices with their start and end apart: 21 -> 17, of which waited for: 10 -> 11; matrix products, arithmetic and copies ran while one was open for 8% -> 3% of each run, Pallas kernels for 6% -> 7%
where the time goes in v4:
time: 166 us; the launch traced here: 165 us
  starting transfers between devices  82.7 us (50%)
  waiting for transfers between devices  55 us (33%)
  Pallas kernels  11.3 us (7%)
  matrix products  5.65 us (3%)
  other arithmetic  4.87 us (3%)
  local copies, waits for them, and re-layouts  2.75 us (2%)
  between operations  2.45 us (1%)
    ppermute x6, starting transfers between devices, stream(): part = join(part, lax.ppermute(part, TENSOR, perm), which)  28.4 us
    ppermute x6, waiting for transfers between devices, stream(): other = lax.ppermute(send, TENSOR, perm)  21.5 us
    all_to_all x1, waiting for transfers between devices, scatter(): out = lax.all_to_all(out, ('y', 'x'), 0, 0, tiled=True)  17.9 us
    all_to_all x1, starting transfers between devices, body(): stats = lax.all_to_all(stats, TENSOR, 0, 0, tiled=True)  14 us
    ppermute x6, starting transfers between devices, stream(): other = lax.ppermute(send, TENSOR, perm)  13.5 us
    ppermute x2, starting transfers between devices, stream(): other = lax.ppermute(part, TENSOR, picks[3][1])  12.1 us
    pallas_call x2, Pallas kernels, perturbed(): pl.pallas_call(perturb_kernel(first, strides, block, 16, (row_names, rows...  11.3 us
    ppermute x1, starting transfers between devices, body(): lax.ppermute(half(out, 1 - z_hi).astype(bf16), 'zh', [(0, 1), (1, 0)])  7.92 us
  transfers between devices with their start and end apart: 17, of which 11 were waited for; matrix products, arithmetic and copies ran while one was open for 3% of the time, Pallas kernels for 7%

profile of v4, /device:TPU:1, one launch (start us, length us, event | category | flops | bytes accessed | tf_op | source)
XLA Modules:
  0.0 164.7 jit_solution(11812165614338721811)
XLA Ops:
  0.6 1.2 convert_reduce_fusion.1
  1.9 1.3 fusion.1
  3.8 14.0 %all-to-all-start = ((f32[16,2,512]{2,1,0:T(2,128)}), f32[16,2,512]{2,1,0:T(2,128)S(1)}, u32[]{:S(2)}, u32[]{:S(2)}) async-start(f32[16,2,512]{2,1,0:T(2,128)} %broadcast_in_dim.2), calls=%async_computation | async-start | bytes 131072 | tf_op jit(solution)/shard_map/all_to_all | solution.py:143
  19.2 5.6 %shard_map.122 = (bf16[576,1152]{1,0:T(8,128)(2,1)}, bf16[576,1152]{1,0:T(8,128)(2,1)}) custom-call(s32[2]{0:T(128)} %seeds.3, s32[3]{0:T(128)} %mults.3, f32[1]{0:T(128)S(6)} %copy.31.step, f32[1]{0:T(128)S(6)} %copy.32.scale, bf16[576,1152]{1,0:T(8,128)(2,1)} %weight.1), custom_call_target="tpu_custom_call" | custom-call | tf_op jit(solution)/shard_map/pallas_call | solution.py:77
  24.9 3.1 %all-to-all-done = f32[16,2,512]{2,1,0:T(2,128)S(1)} async-done(((f32[16,2,512]{2,1,0:T(2,128)}), f32[16,2,512]{2,1,0:T(2,128)S(1)}, u32[]{:S(2)}, u32[]{:S(2)}) %all-to-all-start) | async-done | bytes 65568 | tf_op jit(solution)/shard_map/all_to_all | solution.py:143
  28.3 1.2 convolution_convert_fusion.1
  29.6 2.9 %collective-permute-start = (bf16[256,1152]{1,0:T(8,128)(2,1)S(1)}, bf16[256,1152]{1,0:T(8,128)(2,1)S(1)}, u32[]{:S(2)}, u32[]{:S(2)}) collective-permute-start(bf16[256,1152]{1,0:T(8,128)(2,1)S(1)} %constant_dynamic-slice_fusion.5), channel_id=1, source_target_pairs={{0,1},{1,0},{2,3},{3,2},{4,5},{5,4},{6,7},{7,6},{8,9},{9,8},{10,11... | collective-permute-start | bytes 1769480 | tf_op jit(solution)/shard_map/ppermute | solution.py:163
  32.6 2.5 %convolution_convert_fusion = bf16[512,1152]{1,0:T(8,128)(2,1)S(1)} fusion(bf16[512,576]{0,1:T(8,128)(2,1)S(1)} %fusion.5, bf16[576,1152]{1,0:T(8,128)(2,1)} %get-tuple-element.15), kind=kOutput, calls=%fused_computation | convolution fusion | flops 680067072 | bytes 3096576 | tf_op jit(solution)/shard_map/dot_general | solution.py:160
  35.2 1.9 %collective-permute-start.7 = (bf16[256,1152]{1,0:T(8,128)(2,1)S(1)}, bf16[256,1152]{1,0:T(8,128)(2,1)S(1)}, u32[]{:S(2)}, u32[]{:S(2)}) collective-permute-start(bf16[256,1152]{1,0:T(8,128)(2,1)S(1)} %constant_dynamic-slice_fusion.2), channel_id=1, source_target_pairs={{0,1},{1,0},{2,3},{3,2},{4,5},{5,4},{6,7},{7,6},{8,9},{9,8},{10,11... | collective-permute-start | bytes 1769480 | tf_op jit(solution)/shard_map/ppermute | solution.py:163
  37.3 1.9 %collective-permute-start.1 = (bf16[128,1152]{1,0:T(8,128)(2,1)S(1)}, bf16[128,1152]{1,0:T(8,128)(2,1)S(1)}, u32[]{:S(2)}, u32[]{:S(2)}) collective-permute-start(bf16[128,1152]{1,0:T(8,128)(2,1)S(1)} %constant_dynamic-slice_fusion.4), channel_id=1, source_target_pairs={{0,2},{1,5},{2,0},{3,7},{4,6},{5,1},{6,4},{7,3},{8,10},{9,13},{10,... | collective-permute-start | bytes 884744 | tf_op jit(solution)/shard_map/ppermute | solution.py:163
  39.4 9.3 %collective-permute-done.1 = bf16[128,1152]{1,0:T(8,128)(2,1)S(1)} collective-permute-done((bf16[128,1152]{1,0:T(8,128)(2,1)S(1)}, bf16[128,1152]{1,0:T(8,128)(2,1)S(1)}, u32[]{:S(2)}, u32[]{:S(2)}) %collective-permute-start.1) | collective-permute-done | bytes 294944 | tf_op jit(solution)/shard_map/ppermute | solution.py:163
  48.8 2.0 %collective-permute-start.2 = (bf16[64,1152]{1,0:T(8,128)(2,1)S(1)}, bf16[64,1152]{1,0:T(8,128)(2,1)S(1)}, u32[]{:S(2)}, u32[]{:S(2)}) collective-permute-start(bf16[64,1152]{1,0:T(8,128)(2,1)S(1)} %constant_dynamic-slice_fusion.3), channel_id=1, source_target_pairs={{0,4},{1,3},{2,6},{3,1},{4,0},{5,7},{6,2},{7,5},{8,12},{9,11},{10,... | collective-permute-start | bytes 442376 | tf_op jit(solution)/shard_map/ppermute | solution.py:163
  50.8 2.8 %collective-permute-start.8 = (bf16[128,1152]{1,0:T(8,128)(2,1)S(1)}, bf16[128,1152]{1,0:T(8,128)(2,1)S(1)}, u32[]{:S(2)}, u32[]{:S(2)}) collective-permute-start(bf16[128,1152]{1,0:T(8,128)(2,1)S(1)} %constant_dynamic-slice_fusion.1), channel_id=1, source_target_pairs={{0,2},{1,5},{2,0},{3,7},{4,6},{5,1},{6,4},{7,3},{8,10},{9,13},{10,... | collective-permute-start | bytes 884744 | tf_op jit(solution)/shard_map/ppermute | solution.py:163
  54.7 5.9 %collective-permute-start.3 = (bf16[64,1152]{1,0:T(8,128)(2,1)S(1)}, bf16[64,1152]{1,0:T(8,128)(2,1)S(1)}, u32[]{:S(2)}, u32[]{:S(2)}) collective-permute-start(bf16[64,1152]{1,0:T(8,128)(2,1)S(1)} %add_convert_fusion.5), channel_id=1, source_target_pairs={{0,8},{1,9},{2,10},{3,11},{4,12},{5,13},{6,14},{7,15},{8,0},{9,1},... | collective-permute-start | bytes 442376 | tf_op jit(solution)/shard_map/ppermute | solution.py:166
  60.6 5.4 %collective-permute-done.8 = bf16[128,1152]{1,0:T(8,128)(2,1)S(1)} collective-permute-done((bf16[128,1152]{1,0:T(8,128)(2,1)S(1)}, bf16[128,1152]{1,0:T(8,128)(2,1)S(1)}, u32[]{:S(2)}, u32[]{:S(2)}) %collective-permute-start.8) | collective-permute-done | bytes 294944 | tf_op jit(solution)/shard_map/ppermute | solution.py:163
  66.1 1.9 %collective-permute-start.9 = (bf16[64,1152]{1,0:T(8,128)(2,1)S(1)}, bf16[64,1152]{1,0:T(8,128)(2,1)S(1)}, u32[]{:S(2)}, u32[]{:S(2)}) collective-permute-start(bf16[64,1152]{1,0:T(8,128)(2,1)S(1)} %constant_dynamic-slice_fusion), channel_id=1, source_target_pairs={{0,4},{1,3},{2,6},{3,1},{4,0},{5,7},{6,2},{7,5},{8,12},{9,11},{10,... | collective-permute-start | bytes 442376 | tf_op jit(solution)/shard_map/ppermute | solution.py:163
  68.1 5.9 %collective-permute-done.9 = bf16[64,1152]{1,0:T(8,128)(2,1)S(1)} collective-permute-done((bf16[64,1152]{1,0:T(8,128)(2,1)S(1)}, bf16[64,1152]{1,0:T(8,128)(2,1)S(1)}, u32[]{:S(2)}, u32[]{:S(2)}) %collective-permute-start.9) | collective-permute-done | bytes 147488 | tf_op jit(solution)/shard_map/ppermute | solution.py:163
  74.0 6.2 %collective-permute-start.10 = (bf16[64,1152]{1,0:T(8,128)(2,1)S(1)}, bf16[64,1152]{1,0:T(8,128)(2,1)S(1)}, u32[]{:S(2)}, u32[]{:S(2)}) collective-permute-start(bf16[64,1152]{1,0:T(8,128)(2,1)S(1)} %add_convert_fusion.4), channel_id=1, source_target_pairs={{0,8},{1,9},{2,10},{3,11},{4,12},{5,13},{6,14},{7,15},{8,0},{9,1},... | collective-permute-start | bytes 442376 | tf_op jit(solution)/shard_map/ppermute | solution.py:166
  80.2 1.9 %collective-permute-start.4 = (bf16[64,1152]{1,0:T(8,128)(2,1)S(1)}, bf16[64,1152]{1,0:T(8,128)(2,1)S(1)}, u32[]{:S(2)}, u32[]{:S(2)}) collective-permute-start(bf16[64,1152]{1,0:T(8,128)(2,1)S(1)} %maximum_convert_fusion.1), channel_id=1, source_target_pairs={{0,4},{1,3},{2,6},{3,1},{4,0},{5,7},{6,2},{7,5},{8,12},{9,11},{10,... | collective-permute-start | bytes 442376 | tf_op jit(solution)/shard_map/ppermute | solution.py:170
  82.1 1.7 %collective-permute-done.10 = bf16[64,1152]{1,0:T(8,128)(2,1)S(1)} collective-permute-done((bf16[64,1152]{1,0:T(8,128)(2,1)S(1)}, bf16[64,1152]{1,0:T(8,128)(2,1)S(1)}, u32[]{:S(2)}, u32[]{:S(2)}) %collective-permute-start.10) | collective-permute-done | bytes 147488 | tf_op jit(solution)/shard_map/ppermute | solution.py:166
  83.9 13.8 %collective-permute-start.11 = (bf16[64,1152]{1,0:T(8,128)(2,1)S(1)}, bf16[64,1152]{1,0:T(8,128)(2,1)S(1)}, u32[]{:S(2)}, u32[]{:S(2)}) collective-permute-start(bf16[64,1152]{1,0:T(8,128)(2,1)S(1)} %maximum_convert_fusion), channel_id=1, source_target_pairs={{0,4},{1,3},{2,6},{3,1},{4,0},{5,7},{6,2},{7,5},{8,12},{9,11},{10,... | collective-permute-start | bytes 442376 | tf_op jit(solution)/shard_map/ppermute | solution.py:170
  97.7 1.9 %collective-permute-start.5 = (bf16[128,1152]{1,0:T(8,128)(2,1)S(1)}, bf16[128,1152]{1,0:T(8,128)(2,1)S(1)}, u32[]{:S(2)}, u32[]{:S(2)}) collective-permute-start(bf16[128,1152]{1,0:T(8,128)(2,1)S(1)} %maximum_select_fusion.6), channel_id=1, source_target_pairs={{0,2},{1,5},{2,0},{3,7},{4,6},{5,1},{6,4},{7,3},{8,10},{9,13},{10,... | collective-permute-start | bytes 884744 | tf_op jit(solution)/shard_map/ppermute | solution.py:170
  99.7 5.7 %shard_map.123 = (bf16[576,1152]{1,0:T(8,128)(2,1)}, bf16[576,1152]{1,0:T(8,128)(2,1)}) custom-call(s32[2]{0:T(128)} %seeds.3, s32[3]{0:T(128)} %mults.3, f32[1]{0:T(128)S(6)} %copy.31.step, f32[1]{0:T(128)S(6)} %copy.32.scale, bf16[576,1152]{1,0:T(8,128)(2,1)} %bitcast.22), custom_call_target="tpu_custom_call" | custom-call | tf_op jit(solution)/shard_map/pallas_call | solution.py:77
  105.4 4.4 %collective-permute-start.12 = (bf16[128,1152]{1,0:T(8,128)(2,1)S(1)}, bf16[128,1152]{1,0:T(8,128)(2,1)S(1)}, u32[]{:S(2)}, u32[]{:S(2)}) collective-permute-start(bf16[128,1152]{1,0:T(8,128)(2,1)S(1)} %maximum_select_fusion.7), channel_id=1, source_target_pairs={{0,2},{1,5},{2,0},{3,7},{4,6},{5,1},{6,4},{7,3},{8,10},{9,13},{10,... | collective-permute-start | bytes 884744 | tf_op jit(solution)/shard_map/ppermute | solution.py:170
  110.0 2.6 %collective-permute-start.6 = (bf16[256,1152]{1,0:T(8,128)(2,1)S(1)}, bf16[256,1152]{1,0:T(8,128)(2,1)S(1)}, u32[]{:S(2)}, u32[]{:S(2)}) collective-permute-start(bf16[256,1152]{1,0:T(8,128)(2,1)S(1)} %maximum_select_fusion.4), channel_id=1, source_target_pairs={{0,1},{1,0},{2,3},{3,2},{4,5},{5,4},{6,7},{7,6},{8,9},{9,8},{10,11... | collective-permute-start | bytes 1769480 | tf_op jit(solution)/shard_map/ppermute | solution.py:170
  112.6 4.3 %collective-permute-done.12 = bf16[128,1152]{1,0:T(8,128)(2,1)S(1)} collective-permute-done((bf16[128,1152]{1,0:T(8,128)(2,1)S(1)}, bf16[128,1152]{1,0:T(8,128)(2,1)S(1)}, u32[]{:S(2)}, u32[]{:S(2)}) %collective-permute-start.12) | collective-permute-done | bytes 294944 | tf_op jit(solution)/shard_map/ppermute | solution.py:170
  117.0 3.8 %collective-permute-start.13 = (bf16[256,1152]{1,0:T(8,128)(2,1)S(1)}, bf16[256,1152]{1,0:T(8,128)(2,1)S(1)}, u32[]{:S(2)}, u32[]{:S(2)}) collective-permute-start(bf16[256,1152]{1,0:T(8,128)(2,1)S(1)} %maximum_select_fusion.5), channel_id=1, source_target_pairs={{0,1},{1,0},{2,3},{3,2},{4,5},{5,4},{6,7},{7,6},{8,9},{9,8},{10,11... | collective-permute-start | bytes 1769480 | tf_op jit(solution)/shard_map/ppermute | solution.py:170
  124.2 1.1 copy.21
  125.3 6.8 %all-to-all-start.1 = ((bf16[16,32,1152]{2,1,0:T(8,128)(2,1)}), bf16[16,32,1152]{2,1,0:T(8,128)(2,1)S(1)}, u32[]{:S(2)}, u32[]{:S(2)}) async-start(bf16[16,32,1152]{2,1,0:T(8,128)(2,1)} %bitcast.6), calls=%async_computation.1 | async-start | bytes 2359296 | tf_op jit(solution)/shard_map/all_to_all | solution.py:175
  132.1 17.9 %all-to-all-done.1 = bf16[16,32,1152]{2,1,0:T(8,128)(2,1)S(1)} async-done(((bf16[16,32,1152]{2,1,0:T(8,128)(2,1)}), bf16[16,32,1152]{2,1,0:T(8,128)(2,1)S(1)}, u32[]{:S(2)}, u32[]{:S(2)}) %all-to-all-start.1) | async-done | bytes 1179680 | tf_op jit(solution)/shard_map/all_to_all | solution.py:175
  150.2 7.9 %collective-permute-start.14 = (bf16[16,1152]{1,0:T(8,128)(2,1)S(1)}, bf16[16,1152]{1,0:T(8,128)(2,1)S(1)}, u32[]{:S(2)}, u32[]{:S(2)}) collective-permute-start(bf16[16,1152]{1,0:T(8,128)(2,1)S(1)} %dynamic-slice_convert_fusion), channel_id=1, source_target_pairs={{0,64},{64,0},{1,65},{65,1},{2,66},{66,2},{3,67},{67,3},{4,68},{68... | collective-permute-start | bytes 110600 | tf_op jit(solution)/shard_map/ppermute | solution.py:195
  158.1 5.9 %collective-permute-done.14 = bf16[16,1152]{1,0:T(8,128)(2,1)S(1)} collective-permute-done((bf16[16,1152]{1,0:T(8,128)(2,1)S(1)}, bf16[16,1152]{1,0:T(8,128)(2,1)S(1)}, u32[]{:S(2)}, u32[]{:S(2)}) %collective-permute-start.14) | collective-permute-done | bytes 36896 | tf_op jit(solution)/shard_map/ppermute | solution.py:195
  (63 shorter events, 7.6 us)
Async XLA Ops:
  0.6 18.6 %copy-start.2 = (bf16[576]{0:T(1024)(128)(2,1)S(1)}, bf16[576]{0:T(1024)(128)(2,1)}, u32[]{:S(2)}) copy-start(bf16[576]{0:T(1024)(128)(2,1)} %param.12) | copy-start | bytes 3460
  0.6 18.6 %copy-start.3 = (bf16[576]{0:T(1024)(128)(2,1)S(1)}, bf16[576]{0:T(1024)(128)(2,1)}, u32[]{:S(2)}) copy-start(bf16[576]{0:T(1024)(128)(2,1)} %param.13) | copy-start | bytes 3460
  1.9 26.2 %copy-start = (bf16[512,576]{0,1:T(8,128)(2,1)S(1)}, bf16[512,576]{0,1:T(8,128)(2,1)}, u32[]{:S(2)}) copy-start(bf16[512,576]{0,1:T(8,128)(2,1)} %param.11) | copy-start | bytes 1769476
  3.8 24.1 %all-to-all-start = ((f32[16,2,512]{2,1,0:T(2,128)}), f32[16,2,512]{2,1,0:T(2,128)S(1)}, u32[]{:S(2)}, u32[]{:S(2)}) async-start(f32[16,2,512]{2,1,0:T(2,128)} %broadcast_in_dim.2), calls=%async_computation | async-start | bytes 131072 | tf_op jit(solution)/shard_map/all_to_all | solution.py:143
  24.9 3.5 %copy-start.7 = (bf16[576,1152]{1,0:T(8,128)(2,1)S(1)}, bf16[576,1152]{1,0:T(8,128)(2,1)}, u32[]{:S(2)}) copy-start(bf16[576,1152]{1,0:T(8,128)(2,1)} %get-tuple-element.11) | copy-start | bytes 3981316
  29.6 3.0 %copy-start.1 = (bf16[1152]{0:T(1024)(128)(2,1)S(1)}, bf16[1152]{0:T(1024)(128)(2,1)}, u32[]{:S(2)}) copy-start(bf16[1152]{0:T(1024)(128)(2,1)} %param.15) | copy-start | bytes 6916
  29.6 7.5 %collective-permute-start = (bf16[256,1152]{1,0:T(8,128)(2,1)S(1)}, bf16[256,1152]{1,0:T(8,128)(2,1)S(1)}, u32[]{:S(2)}, u32[]{:S(2)}) collective-permute-start(bf16[256,1152]{1,0:T(8,128)(2,1)S(1)} %constant_dynamic-slice_fusion.5), channel_id=1, source_target_pairs={{0,1},{1,0},{2,3},{3,2},{4,5},{5,4},{6,7},{7,6},{8,9},{9,8},{10,11... | collective-permute-start | bytes 1769480 | tf_op jit(solution)/shard_map/ppermute | solution.py:163
  35.2 4.1 %collective-permute-start.7 = (bf16[256,1152]{1,0:T(8,128)(2,1)S(1)}, bf16[256,1152]{1,0:T(8,128)(2,1)S(1)}, u32[]{:S(2)}, u32[]{:S(2)}) collective-permute-start(bf16[256,1152]{1,0:T(8,128)(2,1)S(1)} %constant_dynamic-slice_fusion.2), channel_id=1, source_target_pairs={{0,1},{1,0},{2,3},{3,2},{4,5},{5,4},{6,7},{7,6},{8,9},{9,8},{10,11... | collective-permute-start | bytes 1769480 | tf_op jit(solution)/shard_map/ppermute | solution.py:163
  37.3 11.4 %collective-permute-start.1 = (bf16[128,1152]{1,0:T(8,128)(2,1)S(1)}, bf16[128,1152]{1,0:T(8,128)(2,1)S(1)}, u32[]{:S(2)}, u32[]{:S(2)}) collective-permute-start(bf16[128,1152]{1,0:T(8,128)(2,1)S(1)} %constant_dynamic-slice_fusion.4), channel_id=1, source_target_pairs={{0,2},{1,5},{2,0},{3,7},{4,6},{5,1},{6,4},{7,3},{8,10},{9,13},{10,... | collective-permute-start | bytes 884744 | tf_op jit(solution)/shard_map/ppermute | solution.py:163
  48.8 5.9 %collective-permute-start.2 = (bf16[64,1152]{1,0:T(8,128)(2,1)S(1)}, bf16[64,1152]{1,0:T(8,128)(2,1)S(1)}, u32[]{:S(2)}, u32[]{:S(2)}) collective-permute-start(bf16[64,1152]{1,0:T(8,128)(2,1)S(1)} %constant_dynamic-slice_fusion.3), channel_id=1, source_target_pairs={{0,4},{1,3},{2,6},{3,1},{4,0},{5,7},{6,2},{7,5},{8,12},{9,11},{10,... | collective-permute-start | bytes 442376 | tf_op jit(solution)/shard_map/ppermute | solution.py:163
  50.8 15.2 %collective-permute-start.8 = (bf16[128,1152]{1,0:T(8,128)(2,1)S(1)}, bf16[128,1152]{1,0:T(8,128)(2,1)S(1)}, u32[]{:S(2)}, u32[]{:S(2)}) collective-permute-start(bf16[128,1152]{1,0:T(8,128)(2,1)S(1)} %constant_dynamic-slice_fusion.1), channel_id=1, source_target_pairs={{0,2},{1,5},{2,0},{3,7},{4,6},{5,1},{6,4},{7,3},{8,10},{9,13},{10,... | collective-permute-start | bytes 884744 | tf_op jit(solution)/shard_map/ppermute | solution.py:163
  54.7 13.3 %collective-permute-start.3 = (bf16[64,1152]{1,0:T(8,128)(2,1)S(1)}, bf16[64,1152]{1,0:T(8,128)(2,1)S(1)}, u32[]{:S(2)}, u32[]{:S(2)}) collective-permute-start(bf16[64,1152]{1,0:T(8,128)(2,1)S(1)} %add_convert_fusion.5), channel_id=1, source_target_pairs={{0,8},{1,9},{2,10},{3,11},{4,12},{5,13},{6,14},{7,15},{8,0},{9,1},... | collective-permute-start | bytes 442376 | tf_op jit(solution)/shard_map/ppermute | solution.py:166
  66.1 7.9 %collective-permute-start.9 = (bf16[64,1152]{1,0:T(8,128)(2,1)S(1)}, bf16[64,1152]{1,0:T(8,128)(2,1)S(1)}, u32[]{:S(2)}, u32[]{:S(2)}) collective-permute-start(bf16[64,1152]{1,0:T(8,128)(2,1)S(1)} %constant_dynamic-slice_fusion), channel_id=1, source_target_pairs={{0,4},{1,3},{2,6},{3,1},{4,0},{5,7},{6,2},{7,5},{8,12},{9,11},{10,... | collective-permute-start | bytes 442376 | tf_op jit(solution)/shard_map/ppermute | solution.py:163
  74.0 9.8 %collective-permute-start.10 = (bf16[64,1152]{1,0:T(8,128)(2,1)S(1)}, bf16[64,1152]{1,0:T(8,128)(2,1)S(1)}, u32[]{:S(2)}, u32[]{:S(2)}) collective-permute-start(bf16[64,1152]{1,0:T(8,128)(2,1)S(1)} %add_convert_fusion.4), channel_id=1, source_target_pairs={{0,8},{1,9},{2,10},{3,11},{4,12},{5,13},{6,14},{7,15},{8,0},{9,1},... | collective-permute-start | bytes 442376 | tf_op jit(solution)/shard_map/ppermute | solution.py:166
  80.2 17.4 %collective-permute-start.4 = (bf16[64,1152]{1,0:T(8,128)(2,1)S(1)}, bf16[64,1152]{1,0:T(8,128)(2,1)S(1)}, u32[]{:S(2)}, u32[]{:S(2)}) collective-permute-start(bf16[64,1152]{1,0:T(8,128)(2,1)S(1)} %maximum_convert_fusion.1), channel_id=1, source_target_pairs={{0,4},{1,3},{2,6},{3,1},{4,0},{5,7},{6,2},{7,5},{8,12},{9,11},{10,... | collective-permute-start | bytes 442376 | tf_op jit(solution)/shard_map/ppermute | solution.py:170
  83.9 21.5 %collective-permute-start.11 = (bf16[64,1152]{1,0:T(8,128)(2,1)S(1)}, bf16[64,1152]{1,0:T(8,128)(2,1)S(1)}, u32[]{:S(2)}, u32[]{:S(2)}) collective-permute-start(bf16[64,1152]{1,0:T(8,128)(2,1)S(1)} %maximum_convert_fusion), channel_id=1, source_target_pairs={{0,4},{1,3},{2,6},{3,1},{4,0},{5,7},{6,2},{7,5},{8,12},{9,11},{10,... | collective-permute-start | bytes 442376 | tf_op jit(solution)/shard_map/ppermute | solution.py:170
  97.7 12.1 %collective-permute-start.5 = (bf16[128,1152]{1,0:T(8,128)(2,1)S(1)}, bf16[128,1152]{1,0:T(8,128)(2,1)S(1)}, u32[]{:S(2)}, u32[]{:S(2)}) collective-permute-start(bf16[128,1152]{1,0:T(8,128)(2,1)S(1)} %maximum_select_fusion.6), channel_id=1, source_target_pairs={{0,2},{1,5},{2,0},{3,7},{4,6},{5,1},{6,4},{7,3},{8,10},{9,13},{10,... | collective-permute-start | bytes 884744 | tf_op jit(solution)/shard_map/ppermute | solution.py:170
  105.4 15.4 %copy-start.6 = (bf16[576,1152]{1,0:T(8,128)(2,1)S(1)}, bf16[576,1152]{1,0:T(8,128)(2,1)}, u32[]{:S(2)}) copy-start(bf16[576,1152]{1,0:T(8,128)(2,1)} %get-tuple-element.13) | copy-start | bytes 3981316
  105.4 11.5 %collective-permute-start.12 = (bf16[128,1152]{1,0:T(8,128)(2,1)S(1)}, bf16[128,1152]{1,0:T(8,128)(2,1)S(1)}, u32[]{:S(2)}, u32[]{:S(2)}) collective-permute-start(bf16[128,1152]{1,0:T(8,128)(2,1)S(1)} %maximum_select_fusion.7), channel_id=1, source_target_pairs={{0,2},{1,5},{2,0},{3,7},{4,6},{5,1},{6,4},{7,3},{8,10},{9,13},{10,... | collective-permute-start | bytes 884744 | tf_op jit(solution)/shard_map/ppermute | solution.py:170
  110.0 10.8 %collective-permute-start.6 = (bf16[256,1152]{1,0:T(8,128)(2,1)S(1)}, bf16[256,1152]{1,0:T(8,128)(2,1)S(1)}, u32[]{:S(2)}, u32[]{:S(2)}) collective-permute-start(bf16[256,1152]{1,0:T(8,128)(2,1)S(1)} %maximum_select_fusion.4), channel_id=1, source_target_pairs={{0,1},{1,0},{2,3},{3,2},{4,5},{5,4},{6,7},{7,6},{8,9},{9,8},{10,11... | collective-permute-start | bytes 1769480 | tf_op jit(solution)/shard_map/ppermute | solution.py:170
  117.0 5.4 %copy-start.5 = (bf16[576,1152]{1,0:T(8,128)(2,1)S(1)}, bf16[576,1152]{1,0:T(8,128)(2,1)}, u32[]{:S(2)}) copy-start(bf16[576,1152]{1,0:T(8,128)(2,1)} %get-tuple-element.19) | copy-start | bytes 3981316
  117.0 5.4 %collective-permute-start.13 = (bf16[256,1152]{1,0:T(8,128)(2,1)S(1)}, bf16[256,1152]{1,0:T(8,128)(2,1)S(1)}, u32[]{:S(2)}, u32[]{:S(2)}) collective-permute-start(bf16[256,1152]{1,0:T(8,128)(2,1)S(1)} %maximum_select_fusion.5), channel_id=1, source_target_pairs={{0,1},{1,0},{2,3},{3,2},{4,5},{5,4},{6,7},{7,6},{8,9},{9,8},{10,11... | collective-permute-start | bytes 1769480 | tf_op jit(solution)/shard_map/ppermute | solution.py:170
  125.3 24.7 %all-to-all-start.1 = ((bf16[16,32,1152]{2,1,0:T(8,128)(2,1)}), bf16[16,32,1152]{2,1,0:T(8,128)(2,1)S(1)}, u32[]{:S(2)}, u32[]{:S(2)}) async-start(bf16[16,32,1152]{2,1,0:T(8,128)(2,1)} %bitcast.6), calls=%async_computation.1 | async-start | bytes 2359296 | tf_op jit(solution)/shard_map/all_to_all | solution.py:175
  132.1 26.1 %copy-start.4 = (bf16[576]{0:T(1024)(128)(2,1)S(1)}, bf16[576]{0:T(1024)(128)(2,1)}, u32[]{:S(2)}) copy-start(bf16[576]{0:T(1024)(128)(2,1)} %param.17) | copy-start | bytes 3460
  150.2 13.8 %collective-permute-start.14 = (bf16[16,1152]{1,0:T(8,128)(2,1)S(1)}, bf16[16,1152]{1,0:T(8,128)(2,1)S(1)}, u32[]{:S(2)}, u32[]{:S(2)}) collective-permute-start(bf16[16,1152]{1,0:T(8,128)(2,1)S(1)} %dynamic-slice_convert_fusion), channel_id=1, source_target_pairs={{0,64},{64,0},{1,65},{65,1},{2,66},{66,2},{3,67},{67,3},{4,68},{68... | collective-permute-start | bytes 110600 | tf_op jit(solution)/shard_map/ppermute | solution.py:195
